TPU v7x, 512 devices: a whole 4x4x16 slice. The times are simulated.
512 devices in a mesh: tensor: 8 (over y, core), adapter: 16 (over z), dp: 4 (over x).
Axes of the slice: x: 4, y: 4, z: 16, core: 2. Of those that a mesh axis runs over, the one named last changes fastest.
Arguments:
- tokens: bfloat16 [16384, 8192], P(('adapter', 'dp'), 'tensor'), may hold values from -6 to 6
- base_projection_weight: bfloat16 [8192, 4096], P('tensor', 'dp'), may hold values from -0.0625 to 0.0625
- adapter_down_weight: bfloat16 [32, 8192, 64], P('adapter', 'tensor'), may hold values from -0.0625 to 0.0625
- adapter_up_weight: bfloat16 [32, 64, 4096], P('adapter', None, 'tensor'), may hold values from -0.75 to 0.75
- adapter_choice_index: int32 [512, 3], P(('adapter', 'dp')), may hold values from 0 to 31, as said below
Outputs:
- adapted: bfloat16 [16384, 4096], P(('adapter', 'dp'), 'tensor')
Inputs may be any that keep to these rules, and one draw needn't show every extreme that they name: `adapter_choice_index`: adapter a is held by index a // 2 of the adapter axis (its owner). Among the 24 entries of the sequences of one device, at most 3 name adapters of one owner, and in every draw one owner is named exactly 3 times by the entries of every device.
All inputs are finite; a program needn't handle non-finite values.
Results may differ from a plain program's by a relative error of at most 0.02.
Values may be sent and summed in bfloat16 or wider, within the bound.
No kernel may reach another device: no remote copies, remote signals or barrier semaphores. Data moves between devices by JAX's collectives and lax.ppermute only.
A program may use at most 64 MiB of HBM per device.

v0:
```python
import jax
import jax.numpy as jnp
from jax import lax
from jax.sharding import PartitionSpec as P


def base_output(tokens, base_projection_weight):
    partial_value = (
        jnp.dot(
            tokens,
            lax.all_gather(base_projection_weight, "dp", axis=1, tiled=True),
            preferred_element_type=jnp.float32,
        )
        .astype(jnp.bfloat16)
        .astype(jnp.float32)
    )
    return lax.psum_scatter(
        partial_value.astype(jnp.bfloat16), "tensor", scatter_dimension=1, tiled=True
    ).astype(jnp.float32)


def adapter_result_rows(tokens, adapter_down_weight, adapter_up_weight, adapter_choice_index):
    row_count, width_portion = tokens.shape
    seq_count = adapter_choice_index.shape[0]
    seq_length = row_count // seq_count
    local_sequence_count = adapter_down_weight.shape[0]
    rank_width_value = adapter_down_weight.shape[2]
    output_portion = adapter_up_weight.shape[2]
    owners = lax.axis_size("adapter")
    capacity = max(2, 6 * seq_count // owners)
    slot_count = owners * capacity
    adapter_list = adapter_choice_index.reshape(-1)
    pair_count = adapter_list.shape[0]
    owner_of = adapter_list // local_sequence_count
    local_index = adapter_list % local_sequence_count
    positions = jnp.arange(pair_count, dtype=jnp.int32)
    earlier = (owner_of[:, None] == owner_of[None, :]) & (positions[None, :] < positions[:, None])
    slot_rank = jnp.sum(earlier.astype(jnp.int32), axis=1)
    slot_of = owner_of * capacity + slot_rank
    select = (jnp.arange(slot_count, dtype=jnp.int32)[:, None] == slot_of[None, :]).astype(
        jnp.bfloat16
    )
    seq_select = select.reshape(slot_count, seq_count, 3).sum(axis=2)
    seq_blocks = tokens.reshape(seq_count, seq_length * width_portion)
    outgoing = jnp.dot(seq_select, seq_blocks, preferred_element_type=jnp.float32).astype(
        jnp.bfloat16
    )
    outgoing = outgoing.reshape(owners, capacity, seq_length, width_portion)
    one_hot = (
        local_index[:, None] == jnp.arange(local_sequence_count, dtype=jnp.int32)[None, :]
    ).astype(jnp.bfloat16)
    adapter_mask = jnp.dot(select, one_hot, preferred_element_type=jnp.float32).astype(jnp.bfloat16)
    adapter_mask = adapter_mask.reshape(owners, capacity, local_sequence_count)
    down_matrix = jnp.transpose(adapter_down_weight, (1, 0, 2)).reshape(
        width_portion, local_sequence_count * rank_width_value
    )
    up_matrix = adapter_up_weight.reshape(local_sequence_count * rank_width_value, output_portion)
    arrived = lax.all_to_all(outgoing, "adapter", split_axis=0, concat_axis=0, tiled=True)
    arrived_mask = lax.all_to_all(adapter_mask, "adapter", split_axis=0, concat_axis=0, tiled=True)
    senders = arrived.shape[0]
    item_count = arrived.shape[1]
    flattened = arrived.reshape(-1, width_portion)
    every_hidden = jnp.dot(flattened, down_matrix, preferred_element_type=jnp.float32)
    every_hidden = every_hidden.reshape(
        senders, item_count, seq_length, local_sequence_count, rank_width_value
    )
    weights_mask = arrived_mask[:, :, None, :, None]
    chosen = jnp.sum(every_hidden * weights_mask.astype(jnp.float32), axis=3)
    summed = lax.psum(chosen.astype(jnp.bfloat16), "tensor")
    spread = (summed[:, :, :, None, :] * weights_mask).reshape(
        -1, local_sequence_count * rank_width_value
    )
    delta_rows = jnp.dot(spread, up_matrix, preferred_element_type=jnp.float32).astype(jnp.bfloat16)
    delta_rows = delta_rows.reshape(senders, item_count, seq_length, output_portion)
    returned = lax.all_to_all(delta_rows, "adapter", split_axis=0, concat_axis=0, tiled=True)
    returned = returned.reshape(slot_count, seq_length * output_portion)
    gathered_sum = jnp.dot(seq_select.T, returned, preferred_element_type=jnp.float32)
    return gathered_sum.reshape(row_count, output_portion)


def local(
    tokens, base_projection_weight, adapter_down_weight, adapter_up_weight, adapter_choice_index
):
    base_sum = base_output(tokens, base_projection_weight)
    adapter_total_sum = adapter_result_rows(
        tokens, adapter_down_weight, adapter_up_weight, adapter_choice_index
    )
    return (base_sum + adapter_total_sum / 3.0).astype(jnp.bfloat16)


def solution(mesh):
    in_specs = (
        P(("adapter", "dp"), "tensor"),
        P("tensor", "dp"),
        P("adapter", "tensor", None),
        P("adapter", None, "tensor"),
        P(("adapter", "dp"), None),
    )
    out_specs = P(("adapter", "dp"), "tensor")
    return jax.shard_map(local, mesh=mesh, in_specs=in_specs, out_specs=out_specs, check_vma=False)
```

profile of v0, /device:TPU:1, one launch (start us, length us, event | category | flops | bytes accessed | tf_op | source)
XLA Modules:
  0.0 352.3 jit_solution(7095717411438507440)
XLA Ops:
  7.4 0.0 copy-start
  7.4 0.8 copy.37
  8.2 0.1 reshape.149
  8.3 0.2 convert_reduce_fusion
  8.5 0.2 convolution_convert_fusion.3
  8.7 0.1 reshape.153
  8.8 0.6 copy.43
  9.4 15.7 %all-to-all-start.1 = ((bf16[16,3,2]{1,2,0:T(2,128)(2,1)}), bf16[16,3,2]{1,2,0:T(2,128)(2,1)S(1)}, u32[]{:S(2)}, u32[]{:S(2)}) async-start(bf16[16,3,2]{1,2,0:T(2,128)(2,1)} %copy.43), calls=%async_computation.2 | async-start | bytes 16384 | tf_op jit(solution)/shard_map/all_to_all | solution.py:59
  25.2 0.1 reduce_sum.33
  25.3 0.1 copy.42
  25.4 0.1 fusion.8
  25.4 1.3 reshape.150
  26.7 1.0 convolution_convert_fusion
  27.7 3.4 copy.49
  31.2 5.2 %all-to-all-done.1 = bf16[16,3,2]{1,2,0:T(2,128)(2,1)S(1)} async-done(((bf16[16,3,2]{1,2,0:T(2,128)(2,1)}), bf16[16,3,2]{1,2,0:T(2,128)(2,1)S(1)}, u32[]{:S(2)}, u32[]{:S(2)}) %all-to-all-start.1) | async-done | bytes 224 | tf_op jit(solution)/shard_map/all_to_all | solution.py:59
  36.4 6.2 %all-to-all-start = ((bf16[16,3,32,1024]{3,2,1,0:T(8,128)(2,1)}), bf16[16,3,32,1024]{3,2,1,0:T(8,128)(2,1)S(1)}, u32[]{:S(2)}, u32[]{:S(2)}) async-start(bf16[16,3,32,1024]{3,2,1,0:T(8,128)(2,1)} %bitcast.18), calls=%async_computation.1 | async-start | bytes 6291456 | tf_op jit(solution)/shard_map/all_to_all | solution.py:58
  42.7 0.0 all-reduce.2.cloned.1.call-start
  42.7 0.1 copy.44
  42.8 0.1 copy.45
  42.9 136.5 %all-to-all-done = bf16[16,3,32,1024]{3,2,1,0:T(8,128)(2,1)S(1)} async-done(((bf16[16,3,32,1024]{3,2,1,0:T(8,128)(2,1)}), bf16[16,3,32,1024]{3,2,1,0:T(8,128)(2,1)S(1)}, u32[]{:S(2)}, u32[]{:S(2)}) %all-to-all-start) | async-done | bytes 3145760 | tf_op jit(solution)/shard_map/all_to_all | solution.py:58
  179.4 0.0 copy-done
  179.4 1.8 multiply_reduce_fusion
  181.3 0.0 copy-start.2
  181.3 0.0 all-reduce.2.cloned.1.call-update
  181.3 0.0 all-gather.2.cloned.1.call-start
  181.4 0.5 all-gather.2.cloned.1.call-update
  181.9 0.2 copy.46
  182.1 75.4 %all-reduce.2.cloned.1.call-done = bf16[16,3,32,64]{3,2,1,0:T(8,128)(2,1)} async-done(((bf16[16,3,32,64]{3,2,1,0:T(8,128)(2,1)}), bf16[16,3,32,64]{3,2,1,0:T(8,128)(2,1)}) %all-reduce.2.cloned.1.call-update) | async-done | bytes 196624 | tf_op jit(solution)/shard_map/psum | solution.py:69
  257.5 1.8 broadcast_multiply_fusion
  259.3 0.0 copy-start.1
  259.3 0.4 mul.48
  259.7 0.0 copy-done.2
  259.7 1.7 convolution_convert_fusion.2
  261.4 11.2 %all-to-all-start.2 = ((bf16[16,3,32,512]{3,2,1,0:T(8,128)(2,1)}), bf16[16,3,32,512]{3,2,1,0:T(8,128)(2,1)S(1)}, u32[]{:S(2)}, u32[]{:S(2)}) async-start(bf16[16,3,32,512]{3,2,1,0:T(8,128)(2,1)} %bitcast.9), calls=%async_computation.3 | async-start | bytes 3145728 | tf_op jit(solution)/shard_map/all_to_all | solution.py:75
  272.6 0.0 reduce-scatter.2.cloned.1.call-start
  272.7 2.5 all-gather.2.cloned.1.call-done
  275.2 0.0 copy-done.1
  275.2 7.1 %convolution_convert_fusion.1 = bf16[256,4096]{1,0:T(8,128)(2,1)} fusion(bf16[256,1024]{1,0:T(8,128)(2,1)S(1)} %copy-done.1, bf16[1024,4096]{1,0:T(8,128)(2,1)} %all-gather.2.cloned.1.call-done), kind=kOutput, calls=%fused_computation.2 | convolution fusion | flops 2148532224 | bytes 11010048 | tf_op jit(solution)/shard_map/dot_general | solution.py:9
  282.3 0.0 reduce-scatter.2.cloned.1.call-update
  282.3 59.5 %all-to-all-done.2 = bf16[16,3,32,512]{3,2,1,0:T(8,128)(2,1)S(1)} async-done(((bf16[16,3,32,512]{3,2,1,0:T(8,128)(2,1)}), bf16[16,3,32,512]{3,2,1,0:T(8,128)(2,1)S(1)}, u32[]{:S(2)}, u32[]{:S(2)}) %all-to-all-start.2) | async-done | bytes 1572896 | tf_op jit(solution)/shard_map/all_to_all | solution.py:75
  341.8 0.9 copy.50
  342.7 0.3 convolution_multiply_fusion
  343.0 0.1 div.32
  343.1 0.0 reduce-scatter.2.cloned.1.call-done
  343.2 1.7 add_convert_fusion
  (3 shorter events, 0.0 us)
Async XLA Ops:
  7.4 172.1 %copy-start = (bf16[2,1024,64]{1,2,0:T(8,128)(2,1)S(1)}, bf16[2,1024,64]{1,2,0:T(8,128)(2,1)}, u32[]{:S(2)}) copy-start(bf16[2,1024,64]{1,2,0:T(8,128)(2,1)} %param.7) | copy-start | bytes 786436
  9.4 27.0 %all-to-all-start.1 = ((bf16[16,3,2]{1,2,0:T(2,128)(2,1)}), bf16[16,3,2]{1,2,0:T(2,128)(2,1)S(1)}, u32[]{:S(2)}, u32[]{:S(2)}) async-start(bf16[16,3,2]{1,2,0:T(2,128)(2,1)} %copy.43), calls=%async_computation.2 | async-start | bytes 16384 | tf_op jit(solution)/shard_map/all_to_all | solution.py:59
  36.4 143.0 %all-to-all-start = ((bf16[16,3,32,1024]{3,2,1,0:T(8,128)(2,1)}), bf16[16,3,32,1024]{3,2,1,0:T(8,128)(2,1)S(1)}, u32[]{:S(2)}, u32[]{:S(2)}) async-start(bf16[16,3,32,1024]{3,2,1,0:T(8,128)(2,1)} %bitcast.18), calls=%async_computation.1 | async-start | bytes 6291456 | tf_op jit(solution)/shard_map/all_to_all | solution.py:58
  42.7 214.8 %all-reduce.2.cloned.1.call-start = ((), (), s32[]{:S(2)}) async-start(), calls=%async_computation.6 | async-start | bytes 786432 | tf_op jit(solution)/shard_map/psum | solution.py:69
  181.3 78.4 %copy-start.2 = (bf16[2,64,512]{2,1,0:T(8,128)(2,1)S(1)}, bf16[2,64,512]{2,1,0:T(8,128)(2,1)}, u32[]{:S(2)}) copy-start(bf16[2,64,512]{2,1,0:T(8,128)(2,1)} %param.8) | copy-start | bytes 393220
  181.3 93.9 %all-gather.2.cloned.1.call-start = ((), (), s32[]{:S(2)}) async-start(), calls=%async_computation.4 | async-start | bytes 10485760 | tf_op jit(solution)/shard_map/all_gather | solution.py:11
  259.3 15.9 %copy-start.1 = (bf16[256,1024]{1,0:T(8,128)(2,1)S(1)}, bf16[256,1024]{1,0:T(8,128)(2,1)}, u32[]{:S(2)}) copy-start(bf16[256,1024]{1,0:T(8,128)(2,1)} %param.5) | copy-start | bytes 1572868
  261.4 80.4 %all-to-all-start.2 = ((bf16[16,3,32,512]{3,2,1,0:T(8,128)(2,1)}), bf16[16,3,32,512]{3,2,1,0:T(8,128)(2,1)S(1)}, u32[]{:S(2)}, u32[]{:S(2)}) async-start(bf16[16,3,32,512]{3,2,1,0:T(8,128)(2,1)} %bitcast.9), calls=%async_computation.3 | async-start | bytes 3145728 | tf_op jit(solution)/shard_map/all_to_all | solution.py:75
  272.6 70.5 %reduce-scatter.2.cloned.1.call-start = ((), (), s32[]{:S(2)}) async-start(), calls=%async_computation.5 | async-start | bytes 2359296 | tf_op jit(solution)/shard_map/reduce_scatter | solution.py:17
Sparse Core Ops, SparseCore 0:
  181.4 76.0 all-reduce.1
  282.5 41.1 reduce-scatter.1
Sparse Core Ops, SparseCore 1:
  184.1 91.0 all-gather.1
where the time goes:
time: 356 us; the launch traced here: 352 us
  waiting for transfers between devices  280 us (79%)
  starting transfers between devices  33.3 us (9%)
  between operations  15 us (4%)
  matrix products  12.2 us (3%)
  local copies, waits for them, and re-layouts  8.26 us (2%)
  other arithmetic  3.87 us (1%)
    all_to_all x1, waiting for transfers between devices, adapter_result_rows(): lax.all_to_all(outgoing, 'adapter', split_axis=0, concat_axis=0, tiled=True)  137 us
    psum x1, waiting for transfers between devices, adapter_result_rows(): summed = lax.psum(chosen.astype(jnp.bfloat16), 'tensor')  75.4 us
    all_to_all x1, waiting for transfers between devices, adapter_result_rows(): lax.all_to_all(delta_rows, 'adapter', split_axis=0, concat_axis=0, tiled=...  59.5 us
    all_to_all x1, starting transfers between devices, adapter_result_rows(): lax.all_to_all(adapter_mask, 'adapter', split_axis=0, concat_axis=0, tile...  15.7 us
    all_to_all x1, starting transfers between devices, adapter_result_rows(): lax.all_to_all(delta_rows, 'adapter', split_axis=0, concat_axis=0, tiled=...  11.2 us
  transfers between devices with their start and end apart: 6, of which 5 were waited for; matrix products, arithmetic and copies ran while one was open for 5% of the time, Pallas kernels for 0%

commit v1 on v0

v1 whole, which is shorter than its diff:
```python
import jax
import jax.numpy as jnp
from jax import lax
from jax.sharding import PartitionSpec as P


def rotate(value, axis, count, step):
    return lax.ppermute(value, axis, [(i, (i - step) % count) for i in range(count)])


def swap_cores(value, count):
    return lax.ppermute(value, "tensor", [(i, i ^ 1) for i in range(count)])


def transposing_pairs(sides, step):
    pairs = []
    for x in range(sides):
        for y in range(sides):
            for core in range(2):
                target = (y + step) % sides
                pairs.append(((2 * y + core) * sides + x, (2 * x + core) * sides + target))
    return pairs


def base_output(tokens, weight):
    tensor_count = lax.axis_size("tensor")
    sides = lax.axis_size("dp")
    tensor_at = lax.axis_index("tensor")
    x = lax.axis_index("dp")
    core, y = tensor_at % 2, tensor_at // 2
    rows = tokens.shape[0]
    half = weight.shape[1] // 2
    others = [rotate(tokens, "dp", sides, step) for step in range(1, sides)]
    gathered = jnp.concatenate([tokens] + others, axis=0)
    weight_kept = lax.dynamic_slice_in_dim(weight, core * half, half, axis=1)
    weight_given = lax.dynamic_slice_in_dim(weight, (1 - core) * half, half, axis=1)
    given = jnp.dot(gathered, weight_given, preferred_element_type=jnp.float32).astype(jnp.bfloat16)
    taken = swap_cores(given, tensor_count)
    kept = jnp.dot(gathered, weight_kept, preferred_element_type=jnp.float32).astype(jnp.bfloat16)
    pair_sum = (kept.astype(jnp.float32) + taken.astype(jnp.float32)).astype(jnp.bfloat16)
    total = None
    for step in range(sides):
        block = (y + step - x + sides) % sides
        piece = lax.dynamic_slice_in_dim(pair_sum, block * rows, rows, axis=0)
        arrived = lax.ppermute(piece, ("tensor", "dp"), transposing_pairs(sides, step))
        arrived = arrived.astype(jnp.float32)
        total = arrived if total is None else total + arrived
    return total


def adapter_output(tokens, down, up, choice):
    tensor_count = lax.axis_size("tensor")
    rows = tokens.shape[0]
    per_sequence = rows // choice.shape[0]
    rank = down.shape[2]
    down_all = lax.all_gather(jnp.transpose(down, (0, 2, 1)), "adapter", axis=0, tiled=True)
    up_all = lax.all_gather(up, "adapter", axis=0, tiled=True)
    adapters = down_all.shape[0]
    down_all = down_all.reshape(adapters * rank, -1)
    up_all = up_all.reshape(adapters * rank, -1)
    choice_of_row = jnp.repeat(choice.T, per_sequence, axis=1)
    mask = choice_of_row[:, None, :] == jnp.arange(adapters, dtype=jnp.int32)[None, :, None]
    every_hidden = lax.dot_general(
        down_all, tokens, (((1,), (1,)), ((), ())), preferred_element_type=jnp.float32
    ).reshape(adapters, rank, rows)
    chosen = [
        jnp.sum(jnp.where(mask[k][:, None, :], every_hidden, 0.0), axis=0) for k in range(3)
    ]
    chosen = jnp.concatenate(chosen, axis=0).astype(jnp.bfloat16)
    pair = chosen.astype(jnp.float32) + swap_cores(chosen, tensor_count).astype(jnp.float32)
    pair = pair.astype(jnp.bfloat16)
    hidden = pair.astype(jnp.float32)
    for step in range(2, tensor_count, 2):
        hidden = hidden + rotate(pair, "tensor", tensor_count, step).astype(jnp.float32)
    hidden = hidden.astype(jnp.bfloat16).reshape(3, 1, rank, rows)
    spread = jnp.sum(
        jnp.where(mask[:, :, None, :], hidden.astype(jnp.float32), 0.0), axis=0
    ).astype(jnp.bfloat16)
    return lax.dot_general(
        spread.reshape(adapters * rank, rows),
        up_all,
        (((0,), (0,)), ((), ())),
        preferred_element_type=jnp.float32,
    )


def local(tokens, base_projection_weight, adapter_down_weight, adapter_up_weight, adapter_choice_index):
    base_sum = base_output(tokens, base_projection_weight)
    delta = adapter_output(tokens, adapter_down_weight, adapter_up_weight, adapter_choice_index)
    return (base_sum + delta / 3.0).astype(jnp.bfloat16)


def solution(mesh):
    in_specs = (
        P(("adapter", "dp"), "tensor"),
        P("tensor", "dp"),
        P("adapter", "tensor", None),
        P("adapter", None, "tensor"),
        P(("adapter", "dp"), None),
    )
    out_specs = P(("adapter", "dp"), "tensor")
    return jax.shard_map(local, mesh=mesh, in_specs=in_specs, out_specs=out_specs, check_vma=False)
```

time: 356 us -> 175 us (0.49)
  the two profiles are of different devices: /device:TPU:1 before, /device:TPU:6 now
where the time goes in v1:
time: 175 us
  waiting for transfers between devices  93.8 us (54%)
  starting transfers between devices  43.7 us (25%)
  matrix products  14.9 us (9%)
  between operations  13.7 us (8%)
  local copies, waits for them, and re-layouts  7.49 us (4%)
    all_gather x1, waiting for transfers between devices, adapter_output(): lax.all_gather(jnp.transpose(down, (0, 2, 1)), 'adapter', axis=0, tiled=T...  42.9 us
    all_gather x1, waiting for transfers between devices, adapter_output(): up_all = lax.all_gather(up, 'adapter', axis=0, tiled=True)  25.2 us
    ppermute x6, starting transfers between devices, rotate(): lax.ppermute(value, axis, [(i, (i - step) % count) for i in range(count)])  25.1 us
    ppermute x4, starting transfers between devices, base_output(): lax.ppermute(piece, ('tensor', 'dp'), transposing_pairs(sides, step))  14.7 us
    ppermute x6, waiting for transfers between devices, rotate(): lax.ppermute(value, axis, [(i, (i - step) % count) for i in range(count)])  12.5 us
    ppermute x4, waiting for transfers between devices, base_output(): lax.ppermute(piece, ('tensor', 'dp'), transposing_pairs(sides, step))  10.8 us
    unnamed x11, local copies, waits for them, and re-layouts  5.7 us
    dot_general x1, matrix products, adapter_output(): lax.dot_general(down_all, tokens, (((1,), (1,)), ((), ())), preferred_ele...  3.95 us
  transfers between devices with their start and end apart: 14, of which 8 were waited for; matrix products, arithmetic and copies ran while one was open for 11% of the time, Pallas kernels for 0%

profile of v1, /device:TPU:6, one launch (start us, length us, event | category | flops | bytes accessed | tf_op | source)
XLA Modules:
  0.0 174.9 jit_solution(1452726102304415098)
XLA Ops:
  6.5 0.0 copy-start
  6.5 0.0 all-gather.3.cloned.1.call-start
  6.5 0.7 all-gather.3.cloned.1.call-update
  7.3 0.0 all-gather.5.cloned.1.call-start
  7.3 0.7 all-gather.5.cloned.1.call-update
  8.0 2.7 %collective-permute-start = (bf16[256,1024]{1,0:T(8,128)(2,1)}, bf16[256,1024]{1,0:T(8,128)(2,1)}, u32[]{:S(2)}, u32[]{:S(2)}) collective-permute-start(bf16[256,1024]{1,0:T(8,128)(2,1)} %param.5), channel_id=1, source_target_pairs={{0,3},{1,0},{2,1},{3,2},{4,7},{5,4},{6,5},{7,6},{8,11},{9,8},{10,9... | collective-permute-start | bytes 1572872 | tf_op jit(solution)/shard_map/ppermute | solution.py:8
  10.8 8.4 %collective-permute-start.1 = (bf16[256,1024]{1,0:T(8,128)(2,1)}, bf16[256,1024]{1,0:T(8,128)(2,1)S(1)}, u32[]{:S(2)}, u32[]{:S(2)}) collective-permute-start(bf16[256,1024]{1,0:T(8,128)(2,1)} %param.5), channel_id=1, source_target_pairs={{0,2},{1,3},{2,0},{3,1},{4,6},{5,7},{6,4},{7,5},{8,10},{9,11},{10,... | collective-permute-start | bytes 1572872 | tf_op jit(solution)/shard_map/ppermute | solution.py:8
  19.2 1.9 %collective-permute-start.2 = (bf16[256,1024]{1,0:T(8,128)(2,1)}, bf16[256,1024]{1,0:T(8,128)(2,1)S(1)}, u32[]{:S(2)}, u32[]{:S(2)}) collective-permute-start(bf16[256,1024]{1,0:T(8,128)(2,1)} %param.5), channel_id=1, source_target_pairs={{0,1},{1,2},{2,3},{3,0},{4,5},{5,6},{6,7},{7,4},{8,9},{9,10},{10,1... | collective-permute-start | bytes 1572872 | tf_op jit(solution)/shard_map/ppermute | solution.py:8
  21.1 1.9 %constant_dynamic-update-slice_fusion.3 = bf16[1024,1024]{1,0:T(8,128)(2,1)} fusion(bf16[256,1024]{1,0:T(8,128)(2,1)} %param.5), kind=kLoop, calls=%fused_computation.25 | loop fusion | bytes 1048576
  23.0 0.8 broadcast_in_dim.55
  23.7 0.1 eq.25
  23.8 12.5 %collective-permute-done = bf16[256,1024]{1,0:T(8,128)(2,1)} collective-permute-done((bf16[256,1024]{1,0:T(8,128)(2,1)}, bf16[256,1024]{1,0:T(8,128)(2,1)}, u32[]{:S(2)}, u32[]{:S(2)}) %collective-permute-start) | collective-permute-done | bytes 524320 | tf_op jit(solution)/shard_map/ppermute | solution.py:8
  36.3 1.9 %constant_dynamic-update-slice_fusion.2 = bf16[1024,1024]{1,0:T(8,128)(2,1)} fusion(bf16[1024,1024]{1,0:T(8,128)(2,1)} %constant_dynamic-update-slice_fusion.3, bf16[256,1024]{1,0:T(8,128)(2,1)} %collective-permute-done), kind=kLoop, calls=%fused_computation.24 | loop fusion | bytes 1048576
  38.2 0.0 collective-permute-done.1
  38.2 0.8 constant_dynamic-update-slice_fusion.1
  39.0 0.0 collective-permute-done.2
  39.0 0.9 constant_dynamic-update-slice_fusion
  39.9 0.0 copy-done
  39.9 3.9 %convolution_convert_fusion = bf16[1024,512]{1,0:T(8,128)(2,1)} fusion(bf16[1024,1024]{1,0:T(8,128)(2,1)} %constant_dynamic-update-slice_fusion, bf16[1024,1024]{1,0:T(8,128)(2,1)S(1)} %copy-done, s32[]{:T(128)S(6)} %select_n.61), kind=kOutput, calls=%fused_computation.5 | convolution fusion | flops 1074266112 | bytes 4194308 | tf_op jit(solution)/shard_map/dot_general | solution.py:37
  43.8 1.9 %collective-permute-start.3 = (bf16[1024,512]{1,0:T(8,128)(2,1)}, bf16[1024,512]{1,0:T(8,128)(2,1)S(1)}, u32[]{:S(2)}, u32[]{:S(2)}) collective-permute-start(bf16[1024,512]{1,0:T(8,128)(2,1)} %convolution_convert_fusion), channel_id=1, source_target_pairs={{0,64},{64,0},{128,192},{192,128},{256,320},{320,256},{384,448},{4... | collective-permute-start | bytes 3145736 | tf_op jit(solution)/shard_map/ppermute | solution.py:12
  45.9 3.8 %convolution_convert_fusion.1 = bf16[1024,512]{1,0:T(8,128)(2,1)} fusion(bf16[1024,1024]{1,0:T(8,128)(2,1)} %constant_dynamic-update-slice_fusion, bf16[1024,1024]{1,0:T(8,128)(2,1)S(1)} %copy-done, s32[]{:T(128)S(6)} %select_n.60), kind=kOutput, calls=%fused_computation.6 | convolution fusion | flops 1074266112 | bytes 4194308 | tf_op jit(solution)/shard_map/dot_general | solution.py:39
  49.7 42.9 %all-gather.3.cloned.1.call-done = bf16[32,64,1024]{2,1,0:T(8,128)(2,1)} async-done(((bf16[2,64,1024]{2,1,0:T(8,128)(2,1)}), bf16[32,64,1024]{2,1,0:T(8,128)(2,1)}) %all-gather.3.cloned.1.call-update) | async-done | bytes 4194320 | tf_op jit(solution)/shard_map/all_gather | solution.py:56
  92.6 0.0 copy-start.1
  92.6 3.9 %select_reduce_fusion.3 = (bf16[64,256]{1,0:T(8,128)(2,1)S(1)}, bf16[64,256]{1,0:T(8,128)(2,1)S(1)}, bf16[64,256]{1,0:T(8,128)(2,1)S(1)}) fusion(pred[32,256]{1,0:T(8,128)(4,1)S(1)} %get-tuple-element.14, pred[32,256]{1,0:T(8,128)(4,1)S(1)} %get-tuple-element.13, pred[32,256]{1,0:T(8,128)(4,1)S(1)} %get-tuple-element.12, ...), kind=kOutput, calls=%fused_computation.3 | convolution fusion | flops 1076838400 | bytes 4841472 | tf_op jit(solution)/shard_map/dot_general | solution.py:63
  96.6 1.9 %collective-permute-start.8 = (bf16[192,256]{1,0:T(8,128)(2,1)S(1)}, bf16[192,256]{1,0:T(8,128)(2,1)S(1)}, u32[]{:S(2)}, u32[]{:S(2)}) collective-permute-start(bf16[192,256]{1,0:T(8,128)(2,1)S(1)} %pad_maximum_fusion), channel_id=1, source_target_pairs={{0,64},{64,0},{128,192},{192,128},{256,320},{320,256},{384,448},{4... | collective-permute-start | bytes 294920 | tf_op jit(solution)/shard_map/ppermute | solution.py:12
  98.5 0.0 collective-permute-done.3
  98.5 0.0 copy-done.1
  98.5 0.3 add_convert_fusion
  98.8 1.0 collective-permute-done.8
  99.8 4.9 %collective-permute-start.10 = (bf16[192,256]{1,0:T(8,128)(2,1)S(1)}, bf16[192,256]{1,0:T(8,128)(2,1)S(1)}, u32[]{:S(2)}, u32[]{:S(2)}) collective-permute-start(bf16[192,256]{1,0:T(8,128)(2,1)S(1)} %add_convert_fusion.3), channel_id=1, source_target_pairs={{0,256},{64,320},{128,384},{192,448},{256,0},{320,64},{384,128},{4... | collective-permute-start | bytes 294920 | tf_op jit(solution)/shard_map/ppermute | solution.py:8
  104.7 2.5 %collective-permute-start.11 = (bf16[192,256]{1,0:T(8,128)(2,1)S(1)}, bf16[192,256]{1,0:T(8,128)(2,1)S(1)}, u32[]{:S(2)}, u32[]{:S(2)}) collective-permute-start(bf16[192,256]{1,0:T(8,128)(2,1)S(1)} %add_convert_fusion.3), channel_id=1, source_target_pairs={{0,128},{64,192},{128,256},{192,320},{256,384},{320,448},{384,0},{... | collective-permute-start | bytes 294920 | tf_op jit(solution)/shard_map/ppermute | solution.py:8
  107.2 4.6 %collective-permute-start.9 = (bf16[192,256]{1,0:T(8,128)(2,1)S(1)}, bf16[192,256]{1,0:T(8,128)(2,1)S(1)}, u32[]{:S(2)}, u32[]{:S(2)}) collective-permute-start(bf16[192,256]{1,0:T(8,128)(2,1)S(1)} %add_convert_fusion.3), channel_id=1, source_target_pairs={{0,384},{64,448},{128,0},{192,64},{256,128},{320,192},{384,256},{4... | collective-permute-start | bytes 294920 | tf_op jit(solution)/shard_map/ppermute | solution.py:8
  111.8 0.1 constant_dynamic-slice_fusion.3
  111.9 1.9 %collective-permute-start.4 = (bf16[256,512]{1,0:T(8,128)(2,1)S(1)}, bf16[256,512]{1,0:T(8,128)(2,1)S(1)}, u32[]{:S(2)}, u32[]{:S(2)}) collective-permute-start(bf16[256,512]{1,0:T(8,128)(2,1)S(1)} %get-tuple-element.8), channel_id=1, source_target_pairs={{0,0},{64,64},{128,1},{192,65},{256,2},{320,66},{384,3},{448,67},{... | collective-permute-start | bytes 786440 | tf_op jit(solution)/shard_map/ppermute | solution.py:45
  113.8 6.3 %collective-permute-start.5 = (bf16[256,512]{1,0:T(8,128)(2,1)S(1)}, bf16[256,512]{1,0:T(8,128)(2,1)S(1)}, u32[]{:S(2)}, u32[]{:S(2)}) collective-permute-start(bf16[256,512]{1,0:T(8,128)(2,1)S(1)} %get-tuple-element.11), channel_id=1, source_target_pairs={{0,1},{64,65},{128,2},{192,66},{256,3},{320,67},{384,0},{448,64},{... | collective-permute-start | bytes 786440 | tf_op jit(solution)/shard_map/ppermute | solution.py:45
  120.2 0.0 collective-permute-done.10
  120.2 4.3 %collective-permute-start.6 = (bf16[256,512]{1,0:T(8,128)(2,1)S(1)}, bf16[256,512]{1,0:T(8,128)(2,1)S(1)}, u32[]{:S(2)}, u32[]{:S(2)}) collective-permute-start(bf16[256,512]{1,0:T(8,128)(2,1)S(1)} %get-tuple-element.10), channel_id=1, source_target_pairs={{0,2},{64,66},{128,3},{192,67},{256,0},{320,64},{384,1},{448,65},{... | collective-permute-start | bytes 786440 | tf_op jit(solution)/shard_map/ppermute | solution.py:45
  124.5 0.0 collective-permute-done.11
  124.5 2.2 %collective-permute-start.7 = (bf16[256,512]{1,0:T(8,128)(2,1)S(1)}, bf16[256,512]{1,0:T(8,128)(2,1)}, u32[]{:S(2)}, u32[]{:S(2)}) collective-permute-start(bf16[256,512]{1,0:T(8,128)(2,1)S(1)} %get-tuple-element.9), channel_id=1, source_target_pairs={{0,3},{64,67},{128,0},{192,64},{256,1},{320,65},{384,2},{448,66},{... | collective-permute-start | bytes 786440 | tf_op jit(solution)/shard_map/ppermute | solution.py:45
  126.7 0.0 collective-permute-done.9
  126.7 0.1 add_convert_fusion.2
  126.8 0.9 select_reduce_fusion
  127.7 3.2 %collective-permute-done.4 = bf16[256,512]{1,0:T(8,128)(2,1)S(1)} collective-permute-done((bf16[256,512]{1,0:T(8,128)(2,1)S(1)}, bf16[256,512]{1,0:T(8,128)(2,1)S(1)}, u32[]{:S(2)}, u32[]{:S(2)}) %collective-permute-start.4) | collective-permute-done | bytes 262176 | tf_op jit(solution)/shard_map/ppermute | solution.py:45
  130.9 2.6 %collective-permute-done.5 = bf16[256,512]{1,0:T(8,128)(2,1)S(1)} collective-permute-done((bf16[256,512]{1,0:T(8,128)(2,1)S(1)}, bf16[256,512]{1,0:T(8,128)(2,1)S(1)}, u32[]{:S(2)}, u32[]{:S(2)}) %collective-permute-start.5) | collective-permute-done | bytes 262176 | tf_op jit(solution)/shard_map/ppermute | solution.py:45
  133.5 0.0 copy-start.2
  133.5 0.3 collective-permute-done.6
  133.8 0.4 copy-done.2
  134.2 0.0 copy-start.3
  134.2 0.7 copy-done.3
  134.9 4.8 %collective-permute-done.7 = bf16[256,512]{1,0:T(8,128)(2,1)} collective-permute-done((bf16[256,512]{1,0:T(8,128)(2,1)S(1)}, bf16[256,512]{1,0:T(8,128)(2,1)}, u32[]{:S(2)}, u32[]{:S(2)}) %collective-permute-start.7) | collective-permute-done | bytes 262176 | tf_op jit(solution)/shard_map/ppermute | solution.py:45
  139.7 25.2 %all-gather.5.cloned.1.call-done = bf16[32,64,512]{2,1,0:T(8,128)(2,1)} async-done(((bf16[2,64,512]{2,1,0:T(8,128)(2,1)}), bf16[32,64,512]{2,1,0:T(8,128)(2,1)}) %all-gather.5.cloned.1.call-update) | async-done | bytes 2097168 | tf_op jit(solution)/shard_map/all_gather | solution.py:57
  164.8 3.2 %add_convert_fusion.1 = bf16[256,512]{1,0:T(8,128)(2,1)} fusion(bf16[256,512]{1,0:T(8,128)(2,1)} %collective-permute-done.7, bf16[256,512]{1,0:T(8,128)(2,1)} %copy-done.3, bf16[256,512]{1,0:T(8,128)(2,1)} %copy-done.2, bf16[256,512]{1,0:T(8,128)(2,1)S(1)} %collective-permute-done.4, bf16[32,64,512]{2,1,0:T(8,128)(2,1)} %all-gather.5.cloned.1.call-done, ...), kind=kOutput, calls=%fused_computation.14 | convolution fusion | flops 538181632 | bytes 4456448 | tf_op jit(solution)/shard_map/dot_general | solution.py:79
  (5 shorter events, 0.1 us)
Async XLA Ops:
  6.5 33.4 %copy-start = (bf16[1024,1024]{1,0:T(8,128)(2,1)S(1)}, bf16[1024,1024]{1,0:T(8,128)(2,1)}, u32[]{:S(2)}) copy-start(bf16[1024,1024]{1,0:T(8,128)(2,1)} %param.6) | copy-start | bytes 6291460
  6.5 86.0 %all-gather.3.cloned.1.call-start = ((), (), s32[]{:S(2)}) async-start(), calls=%async_computation | async-start | bytes 4456448 | tf_op jit(solution)/shard_map/all_gather | solution.py:56
  7.3 157.6 %all-gather.5.cloned.1.call-start = ((), (), s32[]{:S(2)}) async-start(), calls=%async_computation.1 | async-start | bytes 2228224 | tf_op jit(solution)/shard_map/all_gather | solution.py:57
  8.0 28.3 %collective-permute-start = (bf16[256,1024]{1,0:T(8,128)(2,1)}, bf16[256,1024]{1,0:T(8,128)(2,1)}, u32[]{:S(2)}, u32[]{:S(2)}) collective-permute-start(bf16[256,1024]{1,0:T(8,128)(2,1)} %param.5), channel_id=1, source_target_pairs={{0,3},{1,0},{2,1},{3,2},{4,7},{5,4},{6,5},{7,6},{8,11},{9,8},{10,9... | collective-permute-start | bytes 1572872 | tf_op jit(solution)/shard_map/ppermute | solution.py:8
  10.8 27.4 %collective-permute-start.1 = (bf16[256,1024]{1,0:T(8,128)(2,1)}, bf16[256,1024]{1,0:T(8,128)(2,1)S(1)}, u32[]{:S(2)}, u32[]{:S(2)}) collective-permute-start(bf16[256,1024]{1,0:T(8,128)(2,1)} %param.5), channel_id=1, source_target_pairs={{0,2},{1,3},{2,0},{3,1},{4,6},{5,7},{6,4},{7,5},{8,10},{9,11},{10,... | collective-permute-start | bytes 1572872 | tf_op jit(solution)/shard_map/ppermute | solution.py:8
  19.2 19.9 %collective-permute-start.2 = (bf16[256,1024]{1,0:T(8,128)(2,1)}, bf16[256,1024]{1,0:T(8,128)(2,1)S(1)}, u32[]{:S(2)}, u32[]{:S(2)}) collective-permute-start(bf16[256,1024]{1,0:T(8,128)(2,1)} %param.5), channel_id=1, source_target_pairs={{0,1},{1,2},{2,3},{3,0},{4,5},{5,6},{6,7},{7,4},{8,9},{9,10},{10,1... | collective-permute-start | bytes 1572872 | tf_op jit(solution)/shard_map/ppermute | solution.py:8
  43.8 54.6 %collective-permute-start.3 = (bf16[1024,512]{1,0:T(8,128)(2,1)}, bf16[1024,512]{1,0:T(8,128)(2,1)S(1)}, u32[]{:S(2)}, u32[]{:S(2)}) collective-permute-start(bf16[1024,512]{1,0:T(8,128)(2,1)} %convolution_convert_fusion), channel_id=1, source_target_pairs={{0,64},{64,0},{128,192},{192,128},{256,320},{320,256},{384,448},{4... | collective-permute-start | bytes 3145736 | tf_op jit(solution)/shard_map/ppermute | solution.py:12
  92.6 5.9 %copy-start.1 = (bf16[1024,512]{1,0:T(8,128)(2,1)S(1)}, bf16[1024,512]{1,0:T(8,128)(2,1)}, u32[]{:S(2)}) copy-start(bf16[1024,512]{1,0:T(8,128)(2,1)} %convolution_convert_fusion.1) | copy-start | bytes 3145732
  96.6 3.2 %collective-permute-start.8 = (bf16[192,256]{1,0:T(8,128)(2,1)S(1)}, bf16[192,256]{1,0:T(8,128)(2,1)S(1)}, u32[]{:S(2)}, u32[]{:S(2)}) collective-permute-start(bf16[192,256]{1,0:T(8,128)(2,1)S(1)} %pad_maximum_fusion), channel_id=1, source_target_pairs={{0,64},{64,0},{128,192},{192,128},{256,320},{320,256},{384,448},{4... | collective-permute-start | bytes 294920 | tf_op jit(solution)/shard_map/ppermute | solution.py:12
  99.8 20.4 %collective-permute-start.10 = (bf16[192,256]{1,0:T(8,128)(2,1)S(1)}, bf16[192,256]{1,0:T(8,128)(2,1)S(1)}, u32[]{:S(2)}, u32[]{:S(2)}) collective-permute-start(bf16[192,256]{1,0:T(8,128)(2,1)S(1)} %add_convert_fusion.3), channel_id=1, source_target_pairs={{0,256},{64,320},{128,384},{192,448},{256,0},{320,64},{384,128},{4... | collective-permute-start | bytes 294920 | tf_op jit(solution)/shard_map/ppermute | solution.py:8
  104.7 19.8 %collective-permute-start.11 = (bf16[192,256]{1,0:T(8,128)(2,1)S(1)}, bf16[192,256]{1,0:T(8,128)(2,1)S(1)}, u32[]{:S(2)}, u32[]{:S(2)}) collective-permute-start(bf16[192,256]{1,0:T(8,128)(2,1)S(1)} %add_convert_fusion.3), channel_id=1, source_target_pairs={{0,128},{64,192},{128,256},{192,320},{256,384},{320,448},{384,0},{... | collective-permute-start | bytes 294920 | tf_op jit(solution)/shard_map/ppermute | solution.py:8
  107.2 19.5 %collective-permute-start.9 = (bf16[192,256]{1,0:T(8,128)(2,1)S(1)}, bf16[192,256]{1,0:T(8,128)(2,1)S(1)}, u32[]{:S(2)}, u32[]{:S(2)}) collective-permute-start(bf16[192,256]{1,0:T(8,128)(2,1)S(1)} %add_convert_fusion.3), channel_id=1, source_target_pairs={{0,384},{64,448},{128,0},{192,64},{256,128},{320,192},{384,256},{4... | collective-permute-start | bytes 294920 | tf_op jit(solution)/shard_map/ppermute | solution.py:8
  111.9 19.0 %collective-permute-start.4 = (bf16[256,512]{1,0:T(8,128)(2,1)S(1)}, bf16[256,512]{1,0:T(8,128)(2,1)S(1)}, u32[]{:S(2)}, u32[]{:S(2)}) collective-permute-start(bf16[256,512]{1,0:T(8,128)(2,1)S(1)} %get-tuple-element.8), channel_id=1, source_target_pairs={{0,0},{64,64},{128,1},{192,65},{256,2},{320,66},{384,3},{448,67},{... | collective-permute-start | bytes 786440 | tf_op jit(solution)/shard_map/ppermute | solution.py:45
  113.8 19.7 %collective-permute-start.5 = (bf16[256,512]{1,0:T(8,128)(2,1)S(1)}, bf16[256,512]{1,0:T(8,128)(2,1)S(1)}, u32[]{:S(2)}, u32[]{:S(2)}) collective-permute-start(bf16[256,512]{1,0:T(8,128)(2,1)S(1)} %get-tuple-element.11), channel_id=1, source_target_pairs={{0,1},{64,65},{128,2},{192,66},{256,3},{320,67},{384,0},{448,64},{... | collective-permute-start | bytes 786440 | tf_op jit(solution)/shard_map/ppermute | solution.py:45
  120.2 13.6 %collective-permute-start.6 = (bf16[256,512]{1,0:T(8,128)(2,1)S(1)}, bf16[256,512]{1,0:T(8,128)(2,1)S(1)}, u32[]{:S(2)}, u32[]{:S(2)}) collective-permute-start(bf16[256,512]{1,0:T(8,128)(2,1)S(1)} %get-tuple-element.10), channel_id=1, source_target_pairs={{0,2},{64,66},{128,3},{192,67},{256,0},{320,64},{384,1},{448,65},{... | collective-permute-start | bytes 786440 | tf_op jit(solution)/shard_map/ppermute | solution.py:45
  124.5 15.2 %collective-permute-start.7 = (bf16[256,512]{1,0:T(8,128)(2,1)S(1)}, bf16[256,512]{1,0:T(8,128)(2,1)}, u32[]{:S(2)}, u32[]{:S(2)}) collective-permute-start(bf16[256,512]{1,0:T(8,128)(2,1)S(1)} %get-tuple-element.9), channel_id=1, source_target_pairs={{0,3},{64,67},{128,0},{192,64},{256,1},{320,65},{384,2},{448,66},{... | collective-permute-start | bytes 786440 | tf_op jit(solution)/shard_map/ppermute | solution.py:45
  133.5 0.7 copy-start.2
  134.2 0.7 copy-start.3
Sparse Core Ops, SparseCore 0:
  9.4 83.0 all-gather.2
  94.7 70.1 all-gather.4

commit v2 on v1

v2 whole, which is shorter than its diff:
```python
import jax
import jax.numpy as jnp
from jax import lax
from jax.sharding import PartitionSpec as P


def rotate(value, axis, count, step):
    return lax.ppermute(value, axis, [(i, (i - step) % count) for i in range(count)])


def swap_cores(value, count):
    return lax.ppermute(value, "tensor", [(i, i ^ 1) for i in range(count)])


def transposing_pairs(sides, step):
    pairs = []
    for x in range(sides):
        for y in range(sides):
            for core in range(2):
                target = (y + step) % sides
                pairs.append(((2 * y + core) * sides + x, (2 * x + core) * sides + target))
    return pairs


def base_output(gathered, weight):
    tensor_count = lax.axis_size("tensor")
    sides = lax.axis_size("dp")
    tensor_at = lax.axis_index("tensor")
    core, y = tensor_at % 2, tensor_at // 2
    rows = gathered.shape[0] // sides
    half = weight.shape[1] // 2
    weight_kept = lax.dynamic_slice_in_dim(weight, core * half, half, axis=1)
    weight_given = lax.dynamic_slice_in_dim(weight, (1 - core) * half, half, axis=1)
    given = jnp.dot(gathered, weight_given, preferred_element_type=jnp.float32).astype(jnp.bfloat16)
    taken = swap_cores(given, tensor_count)
    kept = jnp.dot(gathered, weight_kept, preferred_element_type=jnp.float32).astype(jnp.bfloat16)
    pair_sum = (kept.astype(jnp.float32) + taken.astype(jnp.float32)).astype(jnp.bfloat16)
    total = None
    for step in range(sides):
        block = (y + step) % sides
        piece = lax.dynamic_slice_in_dim(pair_sum, block * rows, rows, axis=0)
        arrived = lax.ppermute(piece, ("tensor", "dp"), transposing_pairs(sides, step))
        arrived = arrived.astype(jnp.float32)
        total = arrived if total is None else total + arrived
    return total


def choice_mask(choice, per_sequence, adapters):
    of_row = jnp.repeat(choice.T, per_sequence, axis=1)
    return of_row[:, None, None, :] == jnp.arange(adapters, dtype=jnp.int32)[None, :, None, None]


def adapter_output(gathered, down_part, up_parts, choice, choice_all):
    sides = lax.axis_size("dp")
    tensor_count = lax.axis_size("tensor")
    adapters, part, width = down_part.shape
    rows = gathered.shape[0] // sides
    per_sequence = rows // choice.shape[0]
    mask_all = choice_mask(choice_all, per_sequence, adapters)
    every_hidden = lax.dot_general(
        down_part.reshape(adapters * part, width),
        gathered,
        (((1,), (1,)), ((), ())),
        preferred_element_type=jnp.float32,
    ).reshape(adapters, part, sides * rows)
    chosen = [jnp.sum(jnp.where(mask_all[k], every_hidden, 0.0), axis=0) for k in range(3)]
    chosen = jnp.concatenate(chosen, axis=0).astype(jnp.bfloat16)
    pieces = jnp.stack([chosen[:, r * rows : (r + 1) * rows] for r in range(sides)])
    copies = jnp.broadcast_to(pieces[None], (tensor_count,) + pieces.shape)
    copies = copies.reshape((tensor_count * sides,) + pieces.shape[1:])
    arrived = lax.all_to_all(copies, ("tensor", "dp"), 0, 0, tiled=True)
    arrived = arrived.reshape(tensor_count, sides, 3, part, rows)
    hidden = sum(arrived[t].astype(jnp.float32) for t in range(tensor_count)).astype(jnp.bfloat16)
    mask = choice_mask(choice, per_sequence, adapters)
    delta = None
    for q in range(sides):
        spread = sum(
            jnp.where(mask[k], hidden[q, k][None].astype(jnp.float32), 0.0) for k in range(3)
        )
        term = lax.dot_general(
            spread.astype(jnp.bfloat16).reshape(adapters * part, rows),
            up_parts[q],
            (((0,), (0,)), ((), ())),
            preferred_element_type=jnp.float32,
        )
        delta = term if delta is None else delta + term
    return delta


def local(tokens, base_projection_weight, adapter_down_weight, adapter_up_weight, adapter_choice_index):
    sides = lax.axis_size("dp")
    owners = lax.axis_size("adapter")
    x = lax.axis_index("dp")
    held, width, rank = adapter_down_weight.shape
    rows = tokens.shape[0]
    sequences, entries = adapter_choice_index.shape
    part = rank // sides
    own_part = lax.dynamic_slice_in_dim(
        jnp.transpose(adapter_down_weight, (0, 2, 1)), x * part, part, axis=1
    ).reshape(held * part, width)
    up_parts = [
        adapter_up_weight[:, q * part : (q + 1) * part].reshape(held * part, -1)
        for q in range(sides)
    ]
    adapters = lax.all_gather(
        jnp.concatenate([own_part] + up_parts, axis=1), "adapter", axis=0, tiled=True
    )
    note = jnp.pad(
        adapter_choice_index.astype(tokens.dtype), ((0, 16 - sequences), (0, width - entries))
    )
    noted = jnp.concatenate([tokens, note], axis=0)
    gathered = jnp.zeros((sides * rows, width), tokens.dtype)
    choices = jnp.zeros((sides * sequences, entries), jnp.int32)
    for step in range(sides):
        block = noted if step == 0 else rotate(noted, "dp", sides, step)
        place = (x + step) % sides
        gathered = lax.dynamic_update_slice_in_dim(gathered, block[:rows], place * rows, axis=0)
        choice = block[rows : rows + sequences, :entries].astype(jnp.int32)
        choices = lax.dynamic_update_slice_in_dim(choices, choice, place * sequences, axis=0)
    base_sum = base_output(gathered, base_projection_weight)
    adapters, base_sum = lax.optimization_barrier((adapters, base_sum))
    down_part = adapters[:, :width].reshape(owners * held, part, width)
    up_parts = jnp.split(adapters[:, width:], sides, axis=1)
    delta = adapter_output(gathered, down_part, up_parts, adapter_choice_index, choices)
    return (base_sum + delta / 3.0).astype(jnp.bfloat16)


def solution(mesh):
    in_specs = (
        P(("adapter", "dp"), "tensor"),
        P("tensor", "dp"),
        P("adapter", "tensor", None),
        P("adapter", None, "tensor"),
        P(("adapter", "dp"), None),
    )
    out_specs = P(("adapter", "dp"), "tensor")
    return jax.shard_map(local, mesh=mesh, in_specs=in_specs, out_specs=out_specs, check_vma=False)
```

time: 175 us -> 129 us (0.74)
  the two profiles are of different devices: /device:TPU:6 before, /device:TPU:1 now
where the time goes in v2:
time: 129 us; the launch traced here: 128 us
  waiting for transfers between devices  45 us (35%)
  starting transfers between devices  37.3 us (29%)
  between operations  13.9 us (11%)
  local copies, waits for them, and re-layouts  13.2 us (10%)
  matrix products  12.5 us (10%)
  other arithmetic  6.67 us (5%)
    ppermute x3, waiting for transfers between devices, rotate(): lax.ppermute(value, axis, [(i, (i - step) % count) for i in range(count)])  18.8 us
    all_to_all x1, waiting for transfers between devices, adapter_output(): arrived = lax.all_to_all(copies, ('tensor', 'dp'), 0, 0, tiled=True)  13.5 us
    ppermute x4, starting transfers between devices, base_output(): lax.ppermute(piece, ('tensor', 'dp'), transposing_pairs(sides, step))  13.3 us
    ppermute x4, waiting for transfers between devices, base_output(): lax.ppermute(piece, ('tensor', 'dp'), transposing_pairs(sides, step))  12.7 us
    all_to_all x1, starting transfers between devices, adapter_output(): arrived = lax.all_to_all(copies, ('tensor', 'dp'), 0, 0, tiled=True)  11.4 us
    ppermute x3, starting transfers between devices, rotate(): lax.ppermute(value, axis, [(i, (i - step) % count) for i in range(count)])  10.2 us
    dynamic_update_slice x4, local copies, waits for them, and re-layouts, local(): lax.dynamic_update_slice_in_dim(gathered, block[:rows], place * rows, axi...  6.49 us
    dot_general x1, matrix products, base_output(): jnp.dot(gathered, weight_given, preferred_element_type=jnp.float32)  3.86 us
  transfers between devices with their start and end apart: 10, of which 5 were waited for; matrix products, arithmetic and copies ran while one was open for 16% of the time, Pallas kernels for 0%

profile of v2, /device:TPU:1, one launch (start us, length us, event | category | flops | bytes accessed | tf_op | source)
XLA Modules:
  0.0 128.4 jit_solution(777464025743908689)
XLA Ops:
  6.5 1.0 constant_dynamic-slice_fusion.4
  7.5 0.8 fusion.27
  8.4 0.0 copy-start.3
  8.4 0.7 copy-done.3
  9.1 0.0 all-gather.2.cloned.1.call-update
  9.1 0.7 fusion.26
  9.8 0.1 copy.14
  9.9 1.1 fusion.6
  11.0 5.2 %collective-permute-start = (bf16[272,1024]{1,0:T(8,128)(2,1)S(1)}, bf16[272,1024]{1,0:T(8,128)(2,1)}, u32[]{:S(2)}, u32[]{:S(2)}) collective-permute-start(bf16[272,1024]{1,0:T(8,128)(2,1)S(1)} %fusion.6), channel_id=1, source_target_pairs={{0,3},{1,0},{2,1},{3,2},{4,7},{5,4},{6,5},{7,6},{8,11},{9,8},{10,9... | collective-permute-start | bytes 1671176 | tf_op jit(solution)/shard_map/ppermute | solution.py:8
  16.2 2.4 %collective-permute-start.1 = (bf16[272,1024]{1,0:T(8,128)(2,1)S(1)}, bf16[272,1024]{1,0:T(8,128)(2,1)}, u32[]{:S(2)}, u32[]{:S(2)}) collective-permute-start(bf16[272,1024]{1,0:T(8,128)(2,1)S(1)} %fusion.6), channel_id=1, source_target_pairs={{0,2},{1,3},{2,0},{3,1},{4,6},{5,7},{6,4},{7,5},{8,10},{9,11},{10,... | collective-permute-start | bytes 1671176 | tf_op jit(solution)/shard_map/ppermute | solution.py:8
  18.7 2.5 %collective-permute-start.2 = (bf16[272,1024]{1,0:T(8,128)(2,1)S(1)}, bf16[272,1024]{1,0:T(8,128)(2,1)}, u32[]{:S(2)}, u32[]{:S(2)}) collective-permute-start(bf16[272,1024]{1,0:T(8,128)(2,1)S(1)} %fusion.6), channel_id=1, source_target_pairs={{0,1},{1,2},{2,3},{3,0},{4,5},{5,6},{6,7},{7,4},{8,9},{9,10},{10,1... | collective-permute-start | bytes 1671176 | tf_op jit(solution)/shard_map/ppermute | solution.py:8
  21.2 1.6 %broadcast_in_dim.179 = bf16[1024,1024]{1,0:T(8,128)(2,1)} broadcast(bf16[]{:T(256)} %constant.83.clone.1), dimensions={} | broadcast | bytes 2097154 | tf_op jit(solution)/shard_map/broadcast_in_dim | solution.py:112
  22.8 0.8 constant_dynamic-update-slice_fusion.5
  23.7 5.2 %collective-permute-done = bf16[272,1024]{1,0:T(8,128)(2,1)} collective-permute-done((bf16[272,1024]{1,0:T(8,128)(2,1)S(1)}, bf16[272,1024]{1,0:T(8,128)(2,1)}, u32[]{:S(2)}, u32[]{:S(2)}) %collective-permute-start) | collective-permute-done | bytes 557088 | tf_op jit(solution)/shard_map/ppermute | solution.py:8
  28.8 1.9 %slice_dynamic-update-slice_fusion.2 = bf16[1024,1024]{1,0:T(8,128)(2,1)} fusion(bf16[1024,1024]{1,0:T(8,128)(2,1)} %constant_dynamic-update-slice_fusion.5, s32[]{:T(128)S(6)} %select_n.163, bf16[272,1024]{1,0:T(8,128)(2,1)} %collective-permute-done), kind=kLoop, calls=%fused_computation.19 | loop fusion | bytes 1048580 | tf_op jit(solution)/shard_map/dynamic_update_slice | solution.py:117
  30.7 0.0 collective-permute-done.1
  30.7 1.9 %slice_dynamic-update-slice_fusion.1 = bf16[1024,1024]{1,0:T(8,128)(2,1)} fusion(bf16[1024,1024]{1,0:T(8,128)(2,1)} %slice_dynamic-update-slice_fusion.2, s32[]{:T(128)S(6)} %select_n.165, bf16[272,1024]{1,0:T(8,128)(2,1)} %collective-permute-done.1), kind=kLoop, calls=%fused_computation.18 | loop fusion | bytes 1048580 | tf_op jit(solution)/shard_map/dynamic_update_slice | solution.py:117
  32.6 13.6 %collective-permute-done.2 = bf16[272,1024]{1,0:T(8,128)(2,1)} collective-permute-done((bf16[272,1024]{1,0:T(8,128)(2,1)S(1)}, bf16[272,1024]{1,0:T(8,128)(2,1)}, u32[]{:S(2)}, u32[]{:S(2)}) %collective-permute-start.2) | collective-permute-done | bytes 557088 | tf_op jit(solution)/shard_map/ppermute | solution.py:8
  46.2 1.9 %slice_dynamic-update-slice_fusion = bf16[1024,1024]{1,0:T(8,128)(2,1)} fusion(bf16[1024,1024]{1,0:T(8,128)(2,1)} %slice_dynamic-update-slice_fusion.1, s32[]{:T(128)S(6)} %select_n.167, bf16[272,1024]{1,0:T(8,128)(2,1)} %collective-permute-done.2), kind=kLoop, calls=%fused_computation.17 | loop fusion | bytes 1048580 | tf_op jit(solution)/shard_map/dynamic_update_slice | solution.py:117
  48.1 3.9 %convolution_convert_fusion = bf16[1024,512]{1,0:T(8,128)(2,1)} fusion(bf16[1024,1024]{1,0:T(8,128)(2,1)} %slice_dynamic-update-slice_fusion, bf16[1024,1024]{1,0:T(8,128)(2,1)S(1)} %copy-done, s32[]{:T(128)S(6)} %select_n.170), kind=kOutput, calls=%fused_computation.4 | convolution fusion | flops 1074266112 | bytes 4194308 | tf_op jit(solution)/shard_map/dot_general | solution.py:34
  52.0 2.4 %collective-permute-start.3 = (bf16[1024,512]{1,0:T(8,128)(2,1)}, bf16[1024,512]{1,0:T(8,128)(2,1)S(1)}, u32[]{:S(2)}, u32[]{:S(2)}) collective-permute-start(bf16[1024,512]{1,0:T(8,128)(2,1)} %convolution_convert_fusion), channel_id=1, source_target_pairs={{0,64},{64,0},{128,192},{192,128},{256,320},{320,256},{384,448},{4... | collective-permute-start | bytes 3145736 | tf_op jit(solution)/shard_map/ppermute | solution.py:12
  54.5 0.1 dynamic_update_slice.28
  54.7 0.7 slice_convert_fusion
  55.4 0.1 copy.13
  55.4 0.7 slice_convert_fusion.1
  56.1 0.1 copy.12
  56.2 0.7 slice_convert_fusion.2
  56.9 0.1 copy.11
  57.0 0.2 dynamic_update_slice.29
  57.2 0.2 dynamic_update_slice.30
  57.4 0.2 dynamic_update_slice.31
  57.6 0.1 broadcast_in_dim.184
  57.7 0.1 eq.60
  57.8 2.9 %convolution_convert_fusion.1 = bf16[1024,512]{1,0:T(8,128)(2,1)S(1)} fusion(bf16[1024,1024]{1,0:T(8,128)(2,1)} %slice_dynamic-update-slice_fusion, bf16[1024,1024]{1,0:T(8,128)(2,1)S(1)} %copy-done, s32[]{:T(128)S(6)} %select_n.169), kind=kOutput, calls=%fused_computation.5 | convolution fusion | flops 1074266112 | bytes 4194308 | tf_op jit(solution)/shard_map/dot_general | solution.py:36
  60.7 0.0 collective-permute-done.3
  60.7 0.3 add_convert_fusion
  61.0 0.1 constant_dynamic-slice_fusion.3
  61.1 0.7 collective-permute-start.4
  61.8 8.3 %collective-permute-start.7 = (bf16[256,512]{1,0:T(8,128)(2,1)S(1)}, bf16[256,512]{1,0:T(8,128)(2,1)S(1)}, u32[]{:S(2)}, u32[]{:S(2)}) collective-permute-start(bf16[256,512]{1,0:T(8,128)(2,1)S(1)} %get-tuple-element.15), channel_id=1, source_target_pairs={{0,3},{64,67},{128,0},{192,64},{256,1},{320,65},{384,2},{448,66},{... | collective-permute-start | bytes 786440 | tf_op jit(solution)/shard_map/ppermute | solution.py:42
  70.0 2.4 %collective-permute-start.6 = (bf16[256,512]{1,0:T(8,128)(2,1)S(1)}, bf16[256,512]{1,0:T(8,128)(2,1)S(1)}, u32[]{:S(2)}, u32[]{:S(2)}) collective-permute-start(bf16[256,512]{1,0:T(8,128)(2,1)S(1)} %get-tuple-element.16), channel_id=1, source_target_pairs={{0,2},{64,66},{128,3},{192,67},{256,0},{320,64},{384,1},{448,65},{... | collective-permute-start | bytes 786440 | tf_op jit(solution)/shard_map/ppermute | solution.py:42
  72.4 1.9 %collective-permute-start.5 = (bf16[256,512]{1,0:T(8,128)(2,1)S(1)}, bf16[256,512]{1,0:T(8,128)(2,1)S(1)}, u32[]{:S(2)}, u32[]{:S(2)}) collective-permute-start(bf16[256,512]{1,0:T(8,128)(2,1)S(1)} %get-tuple-element.17), channel_id=1, source_target_pairs={{0,1},{64,65},{128,2},{192,66},{256,3},{320,67},{384,0},{448,64},{... | collective-permute-start | bytes 786440 | tf_op jit(solution)/shard_map/ppermute | solution.py:42
  74.4 0.1 iota_compare_fusion.1
  74.4 0.0 collective-permute-done.4
  74.5 6.4 %collective-permute-done.7 = bf16[256,512]{1,0:T(8,128)(2,1)S(1)} collective-permute-done((bf16[256,512]{1,0:T(8,128)(2,1)S(1)}, bf16[256,512]{1,0:T(8,128)(2,1)S(1)}, u32[]{:S(2)}, u32[]{:S(2)}) %collective-permute-start.7) | collective-permute-done | bytes 262176 | tf_op jit(solution)/shard_map/ppermute | solution.py:42
  80.9 0.0 collective-permute-done.6
  80.9 6.3 %collective-permute-done.5 = bf16[256,512]{1,0:T(8,128)(2,1)S(1)} collective-permute-done((bf16[256,512]{1,0:T(8,128)(2,1)S(1)}, bf16[256,512]{1,0:T(8,128)(2,1)S(1)}, u32[]{:S(2)}, u32[]{:S(2)}) %collective-permute-start.5) | collective-permute-done | bytes 262176 | tf_op jit(solution)/shard_map/ppermute | solution.py:42
  87.1 0.1 convert_add_fusion
  87.3 0.0 all-gather.2.cloned.1.call-done
  87.3 3.2 %fusion.2 = f32[512,1024]{1,0:T(8,128)S(1)} fusion(bf16[1024,1024]{1,0:T(8,128)(2,1)} %slice_dynamic-update-slice_fusion, bf16[512,3072]{1,0:T(8,128)(2,1)} %all-gather.2.cloned.1.call-done), kind=kOutput, calls=%fused_computation.12 | convolution fusion | flops 1073741824 | bytes 5242880 | tf_op jit(solution)/shard_map/dot_general | solution.py:60
  90.5 0.9 select_reduce_fusion.2
  91.4 0.0 copy-start.4
  91.4 1.0 broadcast_in_dim.192
  92.4 11.4 %all-to-all-start = ((bf16[32,48,256]{2,1,0:T(8,128)(2,1)}), bf16[32,48,256]{2,1,0:T(8,128)(2,1)S(1)}, u32[]{:S(2)}, u32[]{:S(2)}) async-start(bf16[32,48,256]{2,1,0:T(8,128)(2,1)} %bitcast.103), calls=%async_computation | async-start | bytes 1572864 | tf_op jit(solution)/shard_map/all_to_all | solution.py:71
  103.8 0.1 broadcast_in_dim.180
  103.9 0.1 eq.56
  104.0 13.5 %all-to-all-done = bf16[32,48,256]{2,1,0:T(8,128)(2,1)S(1)} async-done(((bf16[32,48,256]{2,1,0:T(8,128)(2,1)}), bf16[32,48,256]{2,1,0:T(8,128)(2,1)S(1)}, u32[]{:S(2)}, u32[]{:S(2)}) %all-to-all-start) | async-done | bytes 786464 | tf_op jit(solution)/shard_map/all_to_all | solution.py:71
  117.5 0.1 add_convert_fusion.6
  117.6 0.6 add_convert_fusion.2
  118.2 1.6 %fusion.10 = f32[256,512]{1,0:T(8,128)S(1)} fusion(bf16[512,256]{1,0:T(8,128)(2,1)S(1)} %bitcast.108, bf16[512,3072]{1,0:T(8,128)(2,1)} %all-gather.2.cloned.1.call-done), kind=kOutput, calls=%fused_computation.27 | convolution fusion | flops 134217728 | bytes 1310720 | tf_op jit(solution)/shard_map/dot_general | solution.py:80
  119.8 0.0 copy-done.2
  119.8 0.3 convolution_add_fusion.2
  120.1 0.3 convolution_add_fusion.1
  120.5 0.3 fusion
  120.8 0.8 add_convert_fusion.1
  (20 shorter events, 0.1 us)
Async XLA Ops:
  6.5 41.6 %copy-start = (bf16[1024,1024]{1,0:T(8,128)(2,1)S(1)}, bf16[1024,1024]{1,0:T(8,128)(2,1)}, u32[]{:S(2)}) copy-start(bf16[1024,1024]{1,0:T(8,128)(2,1)} %param.6) | copy-start | bytes 6291460
  6.5 80.7 %all-gather.2.cloned.1.call-start = ((), (), s32[]{:S(2)}) async-start(), calls=%async_computation.1 | async-start | bytes 3342336 | tf_op jit(solution)/shard_map/all_gather | solution.py:105
  6.5 16.3 %copy-start.1 = (bf16[256,1024]{1,0:T(8,128)(2,1)S(1)}, bf16[256,1024]{1,0:T(8,128)(2,1)}, u32[]{:S(2)}) copy-start(bf16[256,1024]{1,0:T(8,128)(2,1)} %param.5) | copy-start | bytes 1572868
  8.4 0.7 copy-start.3
  11.0 17.8 %collective-permute-start = (bf16[272,1024]{1,0:T(8,128)(2,1)S(1)}, bf16[272,1024]{1,0:T(8,128)(2,1)}, u32[]{:S(2)}, u32[]{:S(2)}) collective-permute-start(bf16[272,1024]{1,0:T(8,128)(2,1)S(1)} %fusion.6), channel_id=1, source_target_pairs={{0,3},{1,0},{2,1},{3,2},{4,7},{5,4},{6,5},{7,6},{8,11},{9,8},{10,9... | collective-permute-start | bytes 1671176 | tf_op jit(solution)/shard_map/ppermute | solution.py:8
  16.2 14.5 %collective-permute-start.1 = (bf16[272,1024]{1,0:T(8,128)(2,1)S(1)}, bf16[272,1024]{1,0:T(8,128)(2,1)}, u32[]{:S(2)}, u32[]{:S(2)}) collective-permute-start(bf16[272,1024]{1,0:T(8,128)(2,1)S(1)} %fusion.6), channel_id=1, source_target_pairs={{0,2},{1,3},{2,0},{3,1},{4,6},{5,7},{6,4},{7,5},{8,10},{9,11},{10,... | collective-permute-start | bytes 1671176 | tf_op jit(solution)/shard_map/ppermute | solution.py:8
  18.7 27.6 %collective-permute-start.2 = (bf16[272,1024]{1,0:T(8,128)(2,1)S(1)}, bf16[272,1024]{1,0:T(8,128)(2,1)}, u32[]{:S(2)}, u32[]{:S(2)}) collective-permute-start(bf16[272,1024]{1,0:T(8,128)(2,1)S(1)} %fusion.6), channel_id=1, source_target_pairs={{0,1},{1,2},{2,3},{3,0},{4,5},{5,6},{6,7},{7,4},{8,9},{9,10},{10,1... | collective-permute-start | bytes 1671176 | tf_op jit(solution)/shard_map/ppermute | solution.py:8
  52.0 8.7 %collective-permute-start.3 = (bf16[1024,512]{1,0:T(8,128)(2,1)}, bf16[1024,512]{1,0:T(8,128)(2,1)S(1)}, u32[]{:S(2)}, u32[]{:S(2)}) collective-permute-start(bf16[1024,512]{1,0:T(8,128)(2,1)} %convolution_convert_fusion), channel_id=1, source_target_pairs={{0,64},{64,0},{128,192},{192,128},{256,320},{320,256},{384,448},{4... | collective-permute-start | bytes 3145736 | tf_op jit(solution)/shard_map/ppermute | solution.py:12
  61.1 13.4 %collective-permute-start.4 = (bf16[256,512]{1,0:T(8,128)(2,1)S(1)}, bf16[256,512]{1,0:T(8,128)(2,1)S(1)}, u32[]{:S(2)}, u32[]{:S(2)}) collective-permute-start(bf16[256,512]{1,0:T(8,128)(2,1)S(1)} %get-tuple-element.14), channel_id=1, source_target_pairs={{0,0},{64,64},{128,1},{192,65},{256,2},{320,66},{384,3},{448,67},{... | collective-permute-start | bytes 786440 | tf_op jit(solution)/shard_map/ppermute | solution.py:42
  61.8 19.1 %collective-permute-start.7 = (bf16[256,512]{1,0:T(8,128)(2,1)S(1)}, bf16[256,512]{1,0:T(8,128)(2,1)S(1)}, u32[]{:S(2)}, u32[]{:S(2)}) collective-permute-start(bf16[256,512]{1,0:T(8,128)(2,1)S(1)} %get-tuple-element.15), channel_id=1, source_target_pairs={{0,3},{64,67},{128,0},{192,64},{256,1},{320,65},{384,2},{448,66},{... | collective-permute-start | bytes 786440 | tf_op jit(solution)/shard_map/ppermute | solution.py:42
  70.0 10.8 %collective-permute-start.6 = (bf16[256,512]{1,0:T(8,128)(2,1)S(1)}, bf16[256,512]{1,0:T(8,128)(2,1)S(1)}, u32[]{:S(2)}, u32[]{:S(2)}) collective-permute-start(bf16[256,512]{1,0:T(8,128)(2,1)S(1)} %get-tuple-element.16), channel_id=1, source_target_pairs={{0,2},{64,66},{128,3},{192,67},{256,0},{320,64},{384,1},{448,65},{... | collective-permute-start | bytes 786440 | tf_op jit(solution)/shard_map/ppermute | solution.py:42
  72.4 14.7 %collective-permute-start.5 = (bf16[256,512]{1,0:T(8,128)(2,1)S(1)}, bf16[256,512]{1,0:T(8,128)(2,1)S(1)}, u32[]{:S(2)}, u32[]{:S(2)}) collective-permute-start(bf16[256,512]{1,0:T(8,128)(2,1)S(1)} %get-tuple-element.17), channel_id=1, source_target_pairs={{0,1},{64,65},{128,2},{192,66},{256,3},{320,67},{384,0},{448,64},{... | collective-permute-start | bytes 786440 | tf_op jit(solution)/shard_map/ppermute | solution.py:42
  91.4 12.5 %copy-start.4 = (s32[8,3]{0,1:T(4,128)S(1)}, s32[8,3]{0,1:T(4,128)}, u32[]{:S(2)}) copy-start(s32[8,3]{0,1:T(4,128)} %param.9) | copy-start | bytes 292
  92.4 25.1 %all-to-all-start = ((bf16[32,48,256]{2,1,0:T(8,128)(2,1)}), bf16[32,48,256]{2,1,0:T(8,128)(2,1)S(1)}, u32[]{:S(2)}, u32[]{:S(2)}) async-start(bf16[32,48,256]{2,1,0:T(8,128)(2,1)} %bitcast.103), calls=%async_computation | async-start | bytes 1572864 | tf_op jit(solution)/shard_map/all_to_all | solution.py:71
  117.5 2.3 %copy-start.2 = (bf16[512,3072]{1,0:T(8,128)(2,1)S(1)}, bf16[512,3072]{1,0:T(8,128)(2,1)}, u32[]{:S(2)}) copy-start(bf16[512,3072]{1,0:T(8,128)(2,1)} %all-gather.2.cloned.1.call-done) | copy-start | bytes 9437188
Sparse Core Ops, SparseCore 0:
  9.4 73.2 all-gather.1

commit v3 on v2

--- a/solution.py
+++ b/solution.py
@@ -65,12 +65,21 @@
     ).reshape(adapters, part, sides * rows)
     chosen = [jnp.sum(jnp.where(mask_all[k], every_hidden, 0.0), axis=0) for k in range(3)]
     chosen = jnp.concatenate(chosen, axis=0).astype(jnp.bfloat16)
-    pieces = jnp.stack([chosen[:, r * rows : (r + 1) * rows] for r in range(sides)])
-    copies = jnp.broadcast_to(pieces[None], (tensor_count,) + pieces.shape)
-    copies = copies.reshape((tensor_count * sides,) + pieces.shape[1:])
-    arrived = lax.all_to_all(copies, ("tensor", "dp"), 0, 0, tiled=True)
-    arrived = arrived.reshape(tensor_count, sides, 3, part, rows)
-    hidden = sum(arrived[t].astype(jnp.float32) for t in range(tensor_count)).astype(jnp.bfloat16)
+    pair = chosen.astype(jnp.float32) + swap_cores(chosen, tensor_count).astype(jnp.float32)
+    pair = pair.astype(jnp.bfloat16)
+    pieces = jnp.stack([pair[:, r * rows : (r + 1) * rows] for r in range(sides)])
+    chips = tensor_count // 2
+    copies = jnp.broadcast_to(pieces[None], (chips,) + pieces.shape)
+    copies = copies.reshape((chips * sides,) + pieces.shape[1:])
+    groups = [
+        [(2 * y + core) * sides + x for y in range(chips) for x in range(sides)]
+        for core in range(2)
+    ]
+    arrived = lax.all_to_all(
+        copies, ("tensor", "dp"), 0, 0, axis_index_groups=groups, tiled=True
+    )
+    arrived = arrived.reshape(chips, sides, 3, part, rows)
+    hidden = sum(arrived[t].astype(jnp.float32) for t in range(chips)).astype(jnp.bfloat16)
     mask = choice_mask(choice, per_sequence, adapters)
     delta = None
     for q in range(sides):

time: 129 us -> 127 us (0.984)
  waiting for transfers between devices: 45 us -> 41.8 us
  starting transfers between devices: 37.3 us -> 38.8 us
    ppermute x1 -> x2, starting transfers between devices: 2.41 us -> 8.47 us  [swap_cores(): return lax.ppermute(value, 'tensor', [(i, i ^ 1) for i in range(count)])]
    all_to_all x1, starting transfers between devices: 11.4 us -> 6.95 us  [adapter_output(): lax.all_to_all(copies, ('tensor', 'dp'), 0, 0, axis_index_groups=groups,...]
    all_to_all x1, waiting for transfers between devices: 13.5 us -> 9.49 us  [adapter_output(): lax.all_to_all(copies, ('tensor', 'dp'), 0, 0, axis_index_groups=groups,...]
  transfers between devices with their start and end apart: 10 -> 11, of which waited for: 5 -> 6; matrix products, arithmetic and copies ran while one was open for 16% -> 16% of each run, Pallas kernels for 0% -> 0%
where the time goes in v3:
time: 127 us
  waiting for transfers between devices  41.8 us (33%)
  starting transfers between devices  38.8 us (31%)
  between operations  13.9 us (11%)
  local copies, waits for them, and re-layouts  13 us (10%)
  matrix products  12.5 us (10%)
  other arithmetic  6.65 us (5%)
    ppermute x3, waiting for transfers between devices, rotate(): lax.ppermute(value, axis, [(i, (i - step) % count) for i in range(count)])  18.8 us
    ppermute x4, starting transfers between devices, base_output(): lax.ppermute(piece, ('tensor', 'dp'), transposing_pairs(sides, step))  13.3 us
    ppermute x4, waiting for transfers between devices, base_output(): lax.ppermute(piece, ('tensor', 'dp'), transposing_pairs(sides, step))  12.7 us
    ppermute x3, starting transfers between devices, rotate(): lax.ppermute(value, axis, [(i, (i - step) % count) for i in range(count)])  10.2 us
    all_to_all x1, waiting for transfers between devices, adapter_output(): lax.all_to_all(copies, ('tensor', 'dp'), 0, 0, axis_index_groups=groups,...  9.49 us
    ppermute x2, starting transfers between devices, swap_cores(): return lax.ppermute(value, 'tensor', [(i, i ^ 1) for i in range(count)])  8.47 us
    all_to_all x1, starting transfers between devices, adapter_output(): lax.all_to_all(copies, ('tensor', 'dp'), 0, 0, axis_index_groups=groups,...  6.95 us
    dynamic_update_slice x4, local copies, waits for them, and re-layouts, local(): lax.dynamic_update_slice_in_dim(gathered, block[:rows], place * rows, axi...  6.47 us
  transfers between devices with their start and end apart: 11, of which 6 were waited for; matrix products, arithmetic and copies ran while one was open for 16% of the time, Pallas kernels for 0%

profile of v3, /device:TPU:1, one launch (start us, length us, event | category | flops | bytes accessed | tf_op | source)
XLA Modules:
  0.0 126.7 jit_solution(10404417889868699152)
XLA Ops:
  6.5 1.0 constant_dynamic-slice_fusion.4
  7.5 0.8 fusion.27
  8.4 0.0 copy-start.3
  8.4 0.7 copy-done.3
  9.1 0.0 all-gather.2.cloned.1.call-update
  9.1 0.7 fusion.26
  9.8 0.1 copy.14
  9.9 1.1 fusion.6
  11.0 5.2 %collective-permute-start = (bf16[272,1024]{1,0:T(8,128)(2,1)S(1)}, bf16[272,1024]{1,0:T(8,128)(2,1)}, u32[]{:S(2)}, u32[]{:S(2)}) collective-permute-start(bf16[272,1024]{1,0:T(8,128)(2,1)S(1)} %fusion.6), channel_id=1, source_target_pairs={{0,3},{1,0},{2,1},{3,2},{4,7},{5,4},{6,5},{7,6},{8,11},{9,8},{10,9... | collective-permute-start | bytes 1671176 | tf_op jit(solution)/shard_map/ppermute | solution.py:8
  16.2 2.4 %collective-permute-start.1 = (bf16[272,1024]{1,0:T(8,128)(2,1)S(1)}, bf16[272,1024]{1,0:T(8,128)(2,1)}, u32[]{:S(2)}, u32[]{:S(2)}) collective-permute-start(bf16[272,1024]{1,0:T(8,128)(2,1)S(1)} %fusion.6), channel_id=1, source_target_pairs={{0,2},{1,3},{2,0},{3,1},{4,6},{5,7},{6,4},{7,5},{8,10},{9,11},{10,... | collective-permute-start | bytes 1671176 | tf_op jit(solution)/shard_map/ppermute | solution.py:8
  18.7 2.5 %collective-permute-start.2 = (bf16[272,1024]{1,0:T(8,128)(2,1)S(1)}, bf16[272,1024]{1,0:T(8,128)(2,1)}, u32[]{:S(2)}, u32[]{:S(2)}) collective-permute-start(bf16[272,1024]{1,0:T(8,128)(2,1)S(1)} %fusion.6), channel_id=1, source_target_pairs={{0,1},{1,2},{2,3},{3,0},{4,5},{5,6},{6,7},{7,4},{8,9},{9,10},{10,1... | collective-permute-start | bytes 1671176 | tf_op jit(solution)/shard_map/ppermute | solution.py:8
  21.2 1.6 %broadcast_in_dim.179 = bf16[1024,1024]{1,0:T(8,128)(2,1)} broadcast(bf16[]{:T(256)} %constant.83.clone.1), dimensions={} | broadcast | bytes 2097154 | tf_op jit(solution)/shard_map/broadcast_in_dim | solution.py:121
  22.8 0.8 constant_dynamic-update-slice_fusion.5
  23.7 5.2 %collective-permute-done = bf16[272,1024]{1,0:T(8,128)(2,1)} collective-permute-done((bf16[272,1024]{1,0:T(8,128)(2,1)S(1)}, bf16[272,1024]{1,0:T(8,128)(2,1)}, u32[]{:S(2)}, u32[]{:S(2)}) %collective-permute-start) | collective-permute-done | bytes 557088 | tf_op jit(solution)/shard_map/ppermute | solution.py:8
  28.8 1.9 %slice_dynamic-update-slice_fusion.2 = bf16[1024,1024]{1,0:T(8,128)(2,1)} fusion(bf16[1024,1024]{1,0:T(8,128)(2,1)} %constant_dynamic-update-slice_fusion.5, s32[]{:T(128)S(6)} %select_n.163, bf16[272,1024]{1,0:T(8,128)(2,1)} %collective-permute-done), kind=kLoop, calls=%fused_computation.19 | loop fusion | bytes 1048580 | tf_op jit(solution)/shard_map/dynamic_update_slice | solution.py:126
  30.7 1.9 %slice_dynamic-update-slice_fusion.1 = bf16[1024,1024]{1,0:T(8,128)(2,1)} fusion(bf16[1024,1024]{1,0:T(8,128)(2,1)} %slice_dynamic-update-slice_fusion.2, s32[]{:T(128)S(6)} %select_n.165, bf16[272,1024]{1,0:T(8,128)(2,1)} %collective-permute-done.1), kind=kLoop, calls=%fused_computation.18 | loop fusion | bytes 1048580 | tf_op jit(solution)/shard_map/dynamic_update_slice | solution.py:126
  32.6 13.6 %collective-permute-done.2 = bf16[272,1024]{1,0:T(8,128)(2,1)} collective-permute-done((bf16[272,1024]{1,0:T(8,128)(2,1)S(1)}, bf16[272,1024]{1,0:T(8,128)(2,1)}, u32[]{:S(2)}, u32[]{:S(2)}) %collective-permute-start.2) | collective-permute-done | bytes 557088 | tf_op jit(solution)/shard_map/ppermute | solution.py:8
  46.2 1.9 %slice_dynamic-update-slice_fusion = bf16[1024,1024]{1,0:T(8,128)(2,1)} fusion(bf16[1024,1024]{1,0:T(8,128)(2,1)} %slice_dynamic-update-slice_fusion.1, s32[]{:T(128)S(6)} %select_n.167, bf16[272,1024]{1,0:T(8,128)(2,1)} %collective-permute-done.2), kind=kLoop, calls=%fused_computation.17 | loop fusion | bytes 1048580 | tf_op jit(solution)/shard_map/dynamic_update_slice | solution.py:126
  48.1 3.8 %convolution_convert_fusion = bf16[1024,512]{1,0:T(8,128)(2,1)} fusion(bf16[1024,1024]{1,0:T(8,128)(2,1)} %slice_dynamic-update-slice_fusion, bf16[1024,1024]{1,0:T(8,128)(2,1)S(1)} %copy-done, s32[]{:T(128)S(6)} %select_n.170), kind=kOutput, calls=%fused_computation.4 | convolution fusion | flops 1074266112 | bytes 4194308 | tf_op jit(solution)/shard_map/dot_general | solution.py:34
  51.9 2.4 %collective-permute-start.3 = (bf16[1024,512]{1,0:T(8,128)(2,1)}, bf16[1024,512]{1,0:T(8,128)(2,1)S(1)}, u32[]{:S(2)}, u32[]{:S(2)}) collective-permute-start(bf16[1024,512]{1,0:T(8,128)(2,1)} %convolution_convert_fusion), channel_id=1, source_target_pairs={{0,64},{64,0},{128,192},{192,128},{256,320},{320,256},{384,448},{4... | collective-permute-start | bytes 3145736 | tf_op jit(solution)/shard_map/ppermute | solution.py:12
  54.5 0.1 dynamic_update_slice.28
  54.7 0.7 slice_convert_fusion
  55.4 0.1 copy.13
  55.4 0.7 slice_convert_fusion.1
  56.1 0.1 copy.12
  56.2 0.7 slice_convert_fusion.2
  56.9 0.1 copy.11
  57.0 0.2 dynamic_update_slice.29
  57.2 0.2 dynamic_update_slice.30
  57.4 0.2 dynamic_update_slice.31
  57.6 0.1 broadcast_in_dim.184
  57.7 0.1 eq.60
  57.8 2.9 %convolution_convert_fusion.1 = bf16[1024,512]{1,0:T(8,128)(2,1)S(1)} fusion(bf16[1024,1024]{1,0:T(8,128)(2,1)} %slice_dynamic-update-slice_fusion, bf16[1024,1024]{1,0:T(8,128)(2,1)S(1)} %copy-done, s32[]{:T(128)S(6)} %select_n.169), kind=kOutput, calls=%fused_computation.5 | convolution fusion | flops 1074266112 | bytes 4194308 | tf_op jit(solution)/shard_map/dot_general | solution.py:36
  60.7 0.0 collective-permute-done.3
  60.7 0.3 add_convert_fusion
  61.0 0.1 constant_dynamic-slice_fusion.3
  61.1 0.7 collective-permute-start.4
  61.8 8.3 %collective-permute-start.7 = (bf16[256,512]{1,0:T(8,128)(2,1)S(1)}, bf16[256,512]{1,0:T(8,128)(2,1)S(1)}, u32[]{:S(2)}, u32[]{:S(2)}) collective-permute-start(bf16[256,512]{1,0:T(8,128)(2,1)S(1)} %get-tuple-element.15), channel_id=1, source_target_pairs={{0,3},{64,67},{128,0},{192,64},{256,1},{320,65},{384,2},{448,66},{... | collective-permute-start | bytes 786440 | tf_op jit(solution)/shard_map/ppermute | solution.py:42
  70.0 2.4 %collective-permute-start.6 = (bf16[256,512]{1,0:T(8,128)(2,1)S(1)}, bf16[256,512]{1,0:T(8,128)(2,1)S(1)}, u32[]{:S(2)}, u32[]{:S(2)}) collective-permute-start(bf16[256,512]{1,0:T(8,128)(2,1)S(1)} %get-tuple-element.16), channel_id=1, source_target_pairs={{0,2},{64,66},{128,3},{192,67},{256,0},{320,64},{384,1},{448,65},{... | collective-permute-start | bytes 786440 | tf_op jit(solution)/shard_map/ppermute | solution.py:42
  72.4 1.9 %collective-permute-start.5 = (bf16[256,512]{1,0:T(8,128)(2,1)S(1)}, bf16[256,512]{1,0:T(8,128)(2,1)S(1)}, u32[]{:S(2)}, u32[]{:S(2)}) collective-permute-start(bf16[256,512]{1,0:T(8,128)(2,1)S(1)} %get-tuple-element.17), channel_id=1, source_target_pairs={{0,1},{64,65},{128,2},{192,66},{256,3},{320,67},{384,0},{448,64},{... | collective-permute-start | bytes 786440 | tf_op jit(solution)/shard_map/ppermute | solution.py:42
  74.4 0.1 iota_compare_fusion.1
  74.4 0.0 collective-permute-done.4
  74.4 6.4 %collective-permute-done.7 = bf16[256,512]{1,0:T(8,128)(2,1)S(1)} collective-permute-done((bf16[256,512]{1,0:T(8,128)(2,1)S(1)}, bf16[256,512]{1,0:T(8,128)(2,1)S(1)}, u32[]{:S(2)}, u32[]{:S(2)}) %collective-permute-start.7) | collective-permute-done | bytes 262176 | tf_op jit(solution)/shard_map/ppermute | solution.py:42
  80.9 0.0 collective-permute-done.6
  80.9 6.3 %collective-permute-done.5 = bf16[256,512]{1,0:T(8,128)(2,1)S(1)} collective-permute-done((bf16[256,512]{1,0:T(8,128)(2,1)S(1)}, bf16[256,512]{1,0:T(8,128)(2,1)S(1)}, u32[]{:S(2)}, u32[]{:S(2)}) %collective-permute-start.5) | collective-permute-done | bytes 262176 | tf_op jit(solution)/shard_map/ppermute | solution.py:42
  87.1 0.1 convert_add_fusion
  87.3 0.0 all-gather.2.cloned.1.call-done
  87.3 3.2 %fusion.2 = f32[512,1024]{1,0:T(8,128)S(1)} fusion(bf16[1024,1024]{1,0:T(8,128)(2,1)} %slice_dynamic-update-slice_fusion, bf16[512,3072]{1,0:T(8,128)(2,1)} %all-gather.2.cloned.1.call-done), kind=kOutput, calls=%fused_computation.12 | convolution fusion | flops 1073741824 | bytes 5242880 | tf_op jit(solution)/shard_map/dot_general | solution.py:60
  90.5 0.0 copy-start.4
  90.5 0.9 select_reduce_fusion.2
  91.4 6.1 %collective-permute-start.8 = (bf16[48,1024]{1,0:T(8,128)(2,1)S(1)}, bf16[48,1024]{1,0:T(8,128)(2,1)S(1)}, u32[]{:S(2)}, u32[]{:S(2)}) collective-permute-start(bf16[48,1024]{1,0:T(8,128)(2,1)S(1)} %pad_maximum_fusion), channel_id=1, source_target_pairs={{0,64},{64,0},{128,192},{192,128},{256,320},{320,256},{384,448},{4... | collective-permute-start | bytes 294920 | tf_op jit(solution)/shard_map/ppermute | solution.py:12
  97.5 0.1 broadcast_in_dim.180
  97.5 0.1 eq.56
  97.6 0.8 collective-permute-done.8
  98.4 0.8 broadcast_in_dim.192
  99.2 6.9 %all-to-all-start = ((bf16[16,48,256]{2,1,0:T(8,128)(2,1)}), bf16[16,48,256]{2,1,0:T(8,128)(2,1)S(1)}, u32[]{:S(2)}, u32[]{:S(2)}) async-start(bf16[16,48,256]{2,1,0:T(8,128)(2,1)} %bitcast.17), calls=%async_computation | async-start | bytes 786432 | tf_op jit(solution)/shard_map/all_to_all | solution.py:78
  106.2 9.5 %all-to-all-done = bf16[16,48,256]{2,1,0:T(8,128)(2,1)S(1)} async-done(((bf16[16,48,256]{2,1,0:T(8,128)(2,1)}), bf16[16,48,256]{2,1,0:T(8,128)(2,1)S(1)}, u32[]{:S(2)}, u32[]{:S(2)}) %all-to-all-start) | async-done | bytes 393248 | tf_op jit(solution)/shard_map/all_to_all | solution.py:78
  115.7 0.1 add_convert_fusion.6
  115.8 0.6 add_convert_fusion.2
  116.4 1.6 %fusion.10 = f32[256,512]{1,0:T(8,128)S(1)} fusion(bf16[512,256]{1,0:T(8,128)(2,1)S(1)} %bitcast.107, bf16[512,3072]{1,0:T(8,128)(2,1)} %all-gather.2.cloned.1.call-done), kind=kOutput, calls=%fused_computation.27 | convolution fusion | flops 134217728 | bytes 1310720 | tf_op jit(solution)/shard_map/dot_general | solution.py:89
  118.1 0.3 convolution_add_fusion.2
  118.4 0.3 convolution_add_fusion.1
  118.7 0.3 fusion
  119.0 0.8 add_convert_fusion.1
  (23 shorter events, 0.2 us)
Async XLA Ops:
  6.5 41.6 %copy-start = (bf16[1024,1024]{1,0:T(8,128)(2,1)S(1)}, bf16[1024,1024]{1,0:T(8,128)(2,1)}, u32[]{:S(2)}) copy-start(bf16[1024,1024]{1,0:T(8,128)(2,1)} %param.6) | copy-start | bytes 6291460
  6.5 80.7 %all-gather.2.cloned.1.call-start = ((), (), s32[]{:S(2)}) async-start(), calls=%async_computation.1 | async-start | bytes 3342336 | tf_op jit(solution)/shard_map/all_gather | solution.py:114
  6.5 16.3 %copy-start.1 = (bf16[256,1024]{1,0:T(8,128)(2,1)S(1)}, bf16[256,1024]{1,0:T(8,128)(2,1)}, u32[]{:S(2)}) copy-start(bf16[256,1024]{1,0:T(8,128)(2,1)} %param.5) | copy-start | bytes 1572868
  8.4 0.7 copy-start.3
  11.0 17.8 %collective-permute-start = (bf16[272,1024]{1,0:T(8,128)(2,1)S(1)}, bf16[272,1024]{1,0:T(8,128)(2,1)}, u32[]{:S(2)}, u32[]{:S(2)}) collective-permute-start(bf16[272,1024]{1,0:T(8,128)(2,1)S(1)} %fusion.6), channel_id=1, source_target_pairs={{0,3},{1,0},{2,1},{3,2},{4,7},{5,4},{6,5},{7,6},{8,11},{9,8},{10,9... | collective-permute-start | bytes 1671176 | tf_op jit(solution)/shard_map/ppermute | solution.py:8
  16.2 14.5 %collective-permute-start.1 = (bf16[272,1024]{1,0:T(8,128)(2,1)S(1)}, bf16[272,1024]{1,0:T(8,128)(2,1)}, u32[]{:S(2)}, u32[]{:S(2)}) collective-permute-start(bf16[272,1024]{1,0:T(8,128)(2,1)S(1)} %fusion.6), channel_id=1, source_target_pairs={{0,2},{1,3},{2,0},{3,1},{4,6},{5,7},{6,4},{7,5},{8,10},{9,11},{10,... | collective-permute-start | bytes 1671176 | tf_op jit(solution)/shard_map/ppermute | solution.py:8
  18.7 27.6 %collective-permute-start.2 = (bf16[272,1024]{1,0:T(8,128)(2,1)S(1)}, bf16[272,1024]{1,0:T(8,128)(2,1)}, u32[]{:S(2)}, u32[]{:S(2)}) collective-permute-start(bf16[272,1024]{1,0:T(8,128)(2,1)S(1)} %fusion.6), channel_id=1, source_target_pairs={{0,1},{1,2},{2,3},{3,0},{4,5},{5,6},{6,7},{7,4},{8,9},{9,10},{10,1... | collective-permute-start | bytes 1671176 | tf_op jit(solution)/shard_map/ppermute | solution.py:8
  51.9 8.7 %collective-permute-start.3 = (bf16[1024,512]{1,0:T(8,128)(2,1)}, bf16[1024,512]{1,0:T(8,128)(2,1)S(1)}, u32[]{:S(2)}, u32[]{:S(2)}) collective-permute-start(bf16[1024,512]{1,0:T(8,128)(2,1)} %convolution_convert_fusion), channel_id=1, source_target_pairs={{0,64},{64,0},{128,192},{192,128},{256,320},{320,256},{384,448},{4... | collective-permute-start | bytes 3145736 | tf_op jit(solution)/shard_map/ppermute | solution.py:12
  61.1 13.4 %collective-permute-start.4 = (bf16[256,512]{1,0:T(8,128)(2,1)S(1)}, bf16[256,512]{1,0:T(8,128)(2,1)S(1)}, u32[]{:S(2)}, u32[]{:S(2)}) collective-permute-start(bf16[256,512]{1,0:T(8,128)(2,1)S(1)} %get-tuple-element.14), channel_id=1, source_target_pairs={{0,0},{64,64},{128,1},{192,65},{256,2},{320,66},{384,3},{448,67},{... | collective-permute-start | bytes 786440 | tf_op jit(solution)/shard_map/ppermute | solution.py:42
  61.8 19.1 %collective-permute-start.7 = (bf16[256,512]{1,0:T(8,128)(2,1)S(1)}, bf16[256,512]{1,0:T(8,128)(2,1)S(1)}, u32[]{:S(2)}, u32[]{:S(2)}) collective-permute-start(bf16[256,512]{1,0:T(8,128)(2,1)S(1)} %get-tuple-element.15), channel_id=1, source_target_pairs={{0,3},{64,67},{128,0},{192,64},{256,1},{320,65},{384,2},{448,66},{... | collective-permute-start | bytes 786440 | tf_op jit(solution)/shard_map/ppermute | solution.py:42
  70.0 10.8 %collective-permute-start.6 = (bf16[256,512]{1,0:T(8,128)(2,1)S(1)}, bf16[256,512]{1,0:T(8,128)(2,1)S(1)}, u32[]{:S(2)}, u32[]{:S(2)}) collective-permute-start(bf16[256,512]{1,0:T(8,128)(2,1)S(1)} %get-tuple-element.16), channel_id=1, source_target_pairs={{0,2},{64,66},{128,3},{192,67},{256,0},{320,64},{384,1},{448,65},{... | collective-permute-start | bytes 786440 | tf_op jit(solution)/shard_map/ppermute | solution.py:42
  72.4 14.7 %collective-permute-start.5 = (bf16[256,512]{1,0:T(8,128)(2,1)S(1)}, bf16[256,512]{1,0:T(8,128)(2,1)S(1)}, u32[]{:S(2)}, u32[]{:S(2)}) collective-permute-start(bf16[256,512]{1,0:T(8,128)(2,1)S(1)} %get-tuple-element.17), channel_id=1, source_target_pairs={{0,1},{64,65},{128,2},{192,66},{256,3},{320,67},{384,0},{448,64},{... | collective-permute-start | bytes 786440 | tf_op jit(solution)/shard_map/ppermute | solution.py:42
  90.5 7.0 %copy-start.4 = (s32[8,3]{0,1:T(4,128)S(1)}, s32[8,3]{0,1:T(4,128)}, u32[]{:S(2)}) copy-start(s32[8,3]{0,1:T(4,128)} %param.9) | copy-start | bytes 292
  91.4 7.0 %collective-permute-start.8 = (bf16[48,1024]{1,0:T(8,128)(2,1)S(1)}, bf16[48,1024]{1,0:T(8,128)(2,1)S(1)}, u32[]{:S(2)}, u32[]{:S(2)}) collective-permute-start(bf16[48,1024]{1,0:T(8,128)(2,1)S(1)} %pad_maximum_fusion), channel_id=1, source_target_pairs={{0,64},{64,0},{128,192},{192,128},{256,320},{320,256},{384,448},{4... | collective-permute-start | bytes 294920 | tf_op jit(solution)/shard_map/ppermute | solution.py:12
  99.2 16.5 %all-to-all-start = ((bf16[16,48,256]{2,1,0:T(8,128)(2,1)}), bf16[16,48,256]{2,1,0:T(8,128)(2,1)S(1)}, u32[]{:S(2)}, u32[]{:S(2)}) async-start(bf16[16,48,256]{2,1,0:T(8,128)(2,1)} %bitcast.17), calls=%async_computation | async-start | bytes 786432 | tf_op jit(solution)/shard_map/all_to_all | solution.py:78
  115.7 2.3 %copy-start.2 = (bf16[512,3072]{1,0:T(8,128)(2,1)S(1)}, bf16[512,3072]{1,0:T(8,128)(2,1)}, u32[]{:S(2)}) copy-start(bf16[512,3072]{1,0:T(8,128)(2,1)} %all-gather.2.cloned.1.call-done) | copy-start | bytes 9437188
Sparse Core Ops, SparseCore 0:
  9.4 73.3 all-gather.1

commit v4 on v3

--- a/solution.py
+++ b/solution.py
@@ -26,6 +26,7 @@
     tensor_count = lax.axis_size("tensor")
     sides = lax.axis_size("dp")
     tensor_at = lax.axis_index("tensor")
+    x = lax.axis_index("dp")
     core, y = tensor_at % 2, tensor_at // 2
     rows = gathered.shape[0] // sides
     half = weight.shape[1] // 2
@@ -37,7 +38,7 @@
     pair_sum = (kept.astype(jnp.float32) + taken.astype(jnp.float32)).astype(jnp.bfloat16)
     total = None
     for step in range(sides):
-        block = (y + step) % sides
+        block = (y + step - x + sides) % sides
         piece = lax.dynamic_slice_in_dim(pair_sum, block * rows, rows, axis=0)
         arrived = lax.ppermute(piece, ("tensor", "dp"), transposing_pairs(sides, step))
         arrived = arrived.astype(jnp.float32)
@@ -67,7 +68,13 @@
     chosen = jnp.concatenate(chosen, axis=0).astype(jnp.bfloat16)
     pair = chosen.astype(jnp.float32) + swap_cores(chosen, tensor_count).astype(jnp.float32)
     pair = pair.astype(jnp.bfloat16)
-    pieces = jnp.stack([pair[:, r * rows : (r + 1) * rows] for r in range(sides)])
+    x = lax.axis_index("dp")
+    pieces = jnp.stack(
+        [
+            lax.dynamic_slice_in_dim(pair, (r - x + sides) % sides * rows, rows, axis=1)
+            for r in range(sides)
+        ]
+    )
     chips = tensor_count // 2
     copies = jnp.broadcast_to(pieces[None], (chips,) + pieces.shape)
     copies = copies.reshape((chips * sides,) + pieces.shape[1:])
@@ -118,14 +125,13 @@
         adapter_choice_index.astype(tokens.dtype), ((0, 16 - sequences), (0, width - entries))
     )
     noted = jnp.concatenate([tokens, note], axis=0)
-    gathered = jnp.zeros((sides * rows, width), tokens.dtype)
-    choices = jnp.zeros((sides * sequences, entries), jnp.int32)
-    for step in range(sides):
-        block = noted if step == 0 else rotate(noted, "dp", sides, step)
-        place = (x + step) % sides
-        gathered = lax.dynamic_update_slice_in_dim(gathered, block[:rows], place * rows, axis=0)
-        choice = block[rows : rows + sequences, :entries].astype(jnp.int32)
-        choices = lax.dynamic_update_slice_in_dim(choices, choice, place * sequences, axis=0)
+    blocks = [noted] + [rotate(noted, "dp", sides, step) for step in range(1, sides)]
+    gathered = jnp.concatenate([tokens] + [block[:rows] for block in blocks[1:]], axis=0)
+    choices = jnp.concatenate(
+        [adapter_choice_index]
+        + [block[rows : rows + sequences, :entries].astype(jnp.int32) for block in blocks[1:]],
+        axis=0,
+    )
     base_sum = base_output(gathered, base_projection_weight)
     adapters, base_sum = lax.optimization_barrier((adapters, base_sum))
     down_part = adapters[:, :width].reshape(owners * held, part, width)

time: 127 us -> 127 us (level)
  starting transfers between devices: 38.8 us -> 48.3 us
  local copies, waits for them, and re-layouts: 13 us -> 9.62 us
  waiting for transfers between devices: 41.8 us -> 39 us
  matrix products: 12.5 us -> 10.6 us
  other arithmetic: 6.65 us -> 4.77 us
    dynamic_update_slice x8 -> x0, local copies, waits for them, and re-layouts: 7.25 us -> none  [the longest x4 6.47 us: local(): lax.dynamic_update_slice_in_dim(gathered, block[:rows], place * rows, axi...]
    ppermute x2, starting transfers between devices: 8.47 us -> 14.4 us  [swap_cores(): return lax.ppermute(value, 'tensor', [(i, i ^ 1) for i in range(count)])]
    slice x0 -> x6, local copies, waits for them, and re-layouts: none -> 5.45 us  [the longest x3 3.42 us: local(): block[:rows]]
    ppermute x4, starting transfers between devices: 13.3 us -> 15.8 us  [base_output(): lax.ppermute(piece, ('tensor', 'dp'), transposing_pairs(sides, step))]
    convert_element_type x4, other arithmetic: 2.73 us -> 0.71 us  [the longest x1 0.69 us: local(): adapter_choice_index.astype(tokens.dtype)]
    ppermute x4, waiting for transfers between devices: 12.7 us -> 10.8 us  [base_output(): lax.ppermute(piece, ('tensor', 'dp'), transposing_pairs(sides, step))]
    broadcast_in_dim x2 -> x0, local copies, waits for them, and re-layouts: 1.63 us -> none  [the longest x1 1.62 us: local(): gathered = jnp.zeros((sides * rows, width), tokens.dtype)]
    dot_general x1, matrix products: 3.85 us -> 2.24 us  [base_output(): jnp.dot(gathered, weight_given, preferred_element_type=jnp.float32)]
  transfers between devices with their start and end apart: 11 -> 11, of which waited for: 6 -> 7; matrix products, arithmetic and copies ran while one was open for 16% -> 11% of each run, Pallas kernels for 0% -> 0%
where the time goes in v4:
time: 127 us; the launch traced here: 126 us
  starting transfers between devices  48.3 us (38%)
  waiting for transfers between devices  39 us (31%)
  between operations  14 us (11%)
  matrix products  10.6 us (8%)
  local copies, waits for them, and re-layouts  9.62 us (8%)
  other arithmetic  4.77 us (4%)
    ppermute x3, waiting for transfers between devices, rotate(): lax.ppermute(value, axis, [(i, (i - step) % count) for i in range(count)])  18 us
    ppermute x4, starting transfers between devices, base_output(): lax.ppermute(piece, ('tensor', 'dp'), transposing_pairs(sides, step))  15.8 us
    ppermute x2, starting transfers between devices, swap_cores(): return lax.ppermute(value, 'tensor', [(i, i ^ 1) for i in range(count)])  14.4 us
    ppermute x3, starting transfers between devices, rotate(): lax.ppermute(value, axis, [(i, (i - step) % count) for i in range(count)])  11.4 us
    ppermute x4, waiting for transfers between devices, base_output(): lax.ppermute(piece, ('tensor', 'dp'), transposing_pairs(sides, step))  10.8 us
    all_to_all x1, waiting for transfers between devices, adapter_output(): lax.all_to_all(copies, ('tensor', 'dp'), 0, 0, axis_index_groups=groups,...  9.49 us
    all_to_all x1, starting transfers between devices, adapter_output(): lax.all_to_all(copies, ('tensor', 'dp'), 0, 0, axis_index_groups=groups,...  6.72 us
    slice x3, local copies, waits for them, and re-layouts, local(): block[:rows]  3.42 us
  transfers between devices with their start and end apart: 11, of which 7 were waited for; matrix products, arithmetic and copies ran while one was open for 11% of the time, Pallas kernels for 0%

profile of v4, /device:TPU:1, one launch (start us, length us, event | category | flops | bytes accessed | tf_op | source)
XLA Modules:
  0.0 126.2 jit_solution(15884448419260566451)
XLA Ops:
  6.5 0.0 copy-start
  6.5 1.0 constant_dynamic-slice_fusion.4
  7.5 0.8 fusion.26
  8.4 0.0 copy-start.7
  8.4 0.7 copy-done.7
  9.1 0.0 all-gather.2.cloned.1.call-update
  9.1 0.7 convert_element_type.231
  9.8 0.1 copy.24
  9.9 1.1 fusion.6
  11.1 4.0 %collective-permute-start.2 = (bf16[272,1024]{1,0:T(8,128)(2,1)S(1)}, bf16[272,1024]{1,0:T(8,128)(2,1)}, u32[]{:S(2)}, u32[]{:S(2)}) collective-permute-start(bf16[272,1024]{1,0:T(8,128)(2,1)S(1)} %fusion.6), channel_id=1, source_target_pairs={{0,1},{1,2},{2,3},{3,0},{4,5},{5,6},{6,7},{7,4},{8,9},{9,10},{10,1... | collective-permute-start | bytes 1671176 | tf_op jit(solution)/shard_map/ppermute | solution.py:8
  15.0 4.4 %collective-permute-start.1 = (bf16[272,1024]{1,0:T(8,128)(2,1)S(1)}, bf16[272,1024]{1,0:T(8,128)(2,1)}, u32[]{:S(2)}, u32[]{:S(2)}) collective-permute-start(bf16[272,1024]{1,0:T(8,128)(2,1)S(1)} %fusion.6), channel_id=1, source_target_pairs={{0,2},{1,3},{2,0},{3,1},{4,6},{5,7},{6,4},{7,5},{8,10},{9,11},{10,... | collective-permute-start | bytes 1671176 | tf_op jit(solution)/shard_map/ppermute | solution.py:8
  19.4 3.1 %collective-permute-start = (bf16[272,1024]{1,0:T(8,128)(2,1)S(1)}, bf16[272,1024]{1,0:T(8,128)(2,1)}, u32[]{:S(2)}, u32[]{:S(2)}) collective-permute-start(bf16[272,1024]{1,0:T(8,128)(2,1)S(1)} %fusion.6), channel_id=1, source_target_pairs={{0,3},{1,0},{2,1},{3,2},{4,7},{5,4},{6,5},{7,6},{8,11},{9,8},{10,9... | collective-permute-start | bytes 1671176 | tf_op jit(solution)/shard_map/ppermute | solution.py:8
  22.5 0.8 collective-permute-done.2
  23.3 1.1 slice.152
  24.4 17.1 %collective-permute-done.1 = bf16[272,1024]{1,0:T(8,128)(2,1)} collective-permute-done((bf16[272,1024]{1,0:T(8,128)(2,1)S(1)}, bf16[272,1024]{1,0:T(8,128)(2,1)}, u32[]{:S(2)}, u32[]{:S(2)}) %collective-permute-start.1) | collective-permute-done | bytes 557088 | tf_op jit(solution)/shard_map/ppermute | solution.py:8
  41.5 1.1 slice.151
  42.6 0.0 collective-permute-done
  42.6 1.3 %slice.150 = bf16[256,1024]{1,0:T(8,128)(2,1)S(1)} slice(bf16[272,1024]{1,0:T(8,128)(2,1)} %collective-permute-done), slice={[0:256], [0:1024]} | slice | bytes 1048576 | tf_op jit(solution)/shard_map/slice | solution.py:129
  43.9 0.0 copy-start.8
  43.9 2.2 %convolution_convert_fusion = bf16[1024,512]{1,0:T(8,128)(2,1)} fusion(bf16[1024,1024]{1,0:T(8,128)(2,1)S(1)} %copy-done, s32[]{:T(128)S(6)} %select_n.150, bf16[256,1024]{1,0:T(8,128)(2,1)S(1)} %slice.152, bf16[256,1024]{1,0:T(8,128)(2,1)S(1)} %slice.151, bf16[256,1024]{1,0:T(8,128)(2,1)S(1)} %slice.150, bf16[256,1024]{1,0:T(8,128)(2,1)S(1)} %copy-done.2), kind=kOutput, calls=%fused_computation.5 | convolution fusion | flops 1082654720 | bytes 4194308 | tf_op jit(solution)/shard_map/dot_general | solution.py:35
  46.2 0.0 copy-done.4
  46.2 0.0 copy-done.6
  46.2 3.5 %collective-permute-start.3 = (bf16[1024,512]{1,0:T(8,128)(2,1)}, bf16[1024,512]{1,0:T(8,128)(2,1)S(1)}, u32[]{:S(2)}, u32[]{:S(2)}) collective-permute-start(bf16[1024,512]{1,0:T(8,128)(2,1)} %convolution_convert_fusion), channel_id=1, source_target_pairs={{0,64},{64,0},{128,192},{192,128},{256,320},{320,256},{384,448},{4... | collective-permute-start | bytes 3145736 | tf_op jit(solution)/shard_map/ppermute | solution.py:12
  49.8 0.7 slice.156
  50.5 0.1 copy.23
  50.6 0.7 slice.155
  51.3 0.1 copy.22
  51.4 0.7 slice.154
  52.1 0.1 copy.21
  52.2 0.1 add_bitcast_fusion
  52.3 0.1 broadcast_in_dim.176
  52.3 0.1 eq.60
  52.4 2.8 %convolution_convert_fusion.1 = bf16[1024,512]{1,0:T(8,128)(2,1)S(1)} fusion(bf16[1024,1024]{1,0:T(8,128)(2,1)S(1)} %copy-done, s32[]{:T(128)S(6)} %select_n.149, bf16[256,1024]{1,0:T(8,128)(2,1)} %copy-done.4, bf16[256,1024]{1,0:T(8,128)(2,1)} %copy-done.5, bf16[256,1024]{1,0:T(8,128)(2,1)} %copy-done.6, bf16[256,1024]{1,0:T(8,128)(2,1)} %param.5), kind=kOutput, calls=%fused_computation.6 | convolution fusion | flops 1082654720 | bytes 4194308 | tf_op jit(solution)/shard_map/dot_general | solution.py:37
  55.2 0.0 collective-permute-done.3
  55.2 0.3 add_convert_fusion
  55.5 0.0 copy-start.3
  55.5 0.1 constant_dynamic-slice_fusion.3
  55.6 0.8 collective-permute-start.4
  56.4 8.5 %collective-permute-start.7 = (bf16[256,512]{1,0:T(8,128)(2,1)S(1)}, bf16[256,512]{1,0:T(8,128)(2,1)S(1)}, u32[]{:S(2)}, u32[]{:S(2)}) collective-permute-start(bf16[256,512]{1,0:T(8,128)(2,1)S(1)} %get-tuple-element.13), channel_id=1, source_target_pairs={{0,3},{64,67},{128,0},{192,64},{256,1},{320,65},{384,2},{448,66},{... | collective-permute-start | bytes 786440 | tf_op jit(solution)/shard_map/ppermute | solution.py:43
  64.9 4.3 %collective-permute-start.6 = (bf16[256,512]{1,0:T(8,128)(2,1)S(1)}, bf16[256,512]{1,0:T(8,128)(2,1)S(1)}, u32[]{:S(2)}, u32[]{:S(2)}) collective-permute-start(bf16[256,512]{1,0:T(8,128)(2,1)S(1)} %get-tuple-element.14), channel_id=1, source_target_pairs={{0,2},{64,66},{128,3},{192,67},{256,0},{320,64},{384,1},{448,65},{... | collective-permute-start | bytes 786440 | tf_op jit(solution)/shard_map/ppermute | solution.py:43
  69.3 2.2 %collective-permute-start.5 = (bf16[256,512]{1,0:T(8,128)(2,1)S(1)}, bf16[256,512]{1,0:T(8,128)(2,1)S(1)}, u32[]{:S(2)}, u32[]{:S(2)}) collective-permute-start(bf16[256,512]{1,0:T(8,128)(2,1)S(1)} %get-tuple-element.15), channel_id=1, source_target_pairs={{0,1},{64,65},{128,2},{192,66},{256,3},{320,67},{384,0},{448,64},{... | collective-permute-start | bytes 786440 | tf_op jit(solution)/shard_map/ppermute | solution.py:43
  71.5 0.1 iota_compare_fusion.1
  71.5 0.0 collective-permute-done.4
  71.5 4.0 %collective-permute-done.7 = bf16[256,512]{1,0:T(8,128)(2,1)S(1)} collective-permute-done((bf16[256,512]{1,0:T(8,128)(2,1)S(1)}, bf16[256,512]{1,0:T(8,128)(2,1)S(1)}, u32[]{:S(2)}, u32[]{:S(2)}) %collective-permute-start.7) | collective-permute-done | bytes 262176 | tf_op jit(solution)/shard_map/ppermute | solution.py:43
  75.6 0.2 collective-permute-done.6
  75.7 6.6 %collective-permute-done.5 = bf16[256,512]{1,0:T(8,128)(2,1)S(1)} collective-permute-done((bf16[256,512]{1,0:T(8,128)(2,1)S(1)}, bf16[256,512]{1,0:T(8,128)(2,1)S(1)}, u32[]{:S(2)}, u32[]{:S(2)}) %collective-permute-start.5) | collective-permute-done | bytes 262176 | tf_op jit(solution)/shard_map/ppermute | solution.py:43
  82.4 0.1 convert_add_fusion
  82.5 0.0 all-gather.2.cloned.1.call-done
  82.5 3.0 %fusion.2 = f32[512,1024]{1,0:T(8,128)S(1)} fusion(bf16[512,3072]{1,0:T(8,128)(2,1)} %all-gather.2.cloned.1.call-done, bf16[256,1024]{1,0:T(8,128)(2,1)} %copy-done.4, bf16[256,1024]{1,0:T(8,128)(2,1)} %copy-done.5, bf16[256,1024]{1,0:T(8,128)(2,1)} %copy-done.6, bf16[256,1024]{1,0:T(8,128)(2,1)S(1)} %copy-done.3), kind=kOutput, calls=%fused_computation.13 | convolution fusion | flops 1082130432 | bytes 5242880 | tf_op jit(solution)/shard_map/dot_general | solution.py:61
  85.5 0.9 select_reduce_fusion.2
  86.4 10.9 %collective-permute-start.8 = (bf16[48,1024]{1,0:T(8,128)(2,1)S(1)}, bf16[48,1024]{1,0:T(8,128)(2,1)S(1)}, u32[]{:S(2)}, u32[]{:S(2)}) collective-permute-start(bf16[48,1024]{1,0:T(8,128)(2,1)S(1)} %pad_maximum_fusion.1), channel_id=1, source_target_pairs={{0,64},{64,0},{128,192},{192,128},{256,320},{320,256},{384,448},{4... | collective-permute-start | bytes 294920 | tf_op jit(solution)/shard_map/ppermute | solution.py:12
  97.3 0.1 broadcast_in_dim.173
  97.4 0.1 eq.56
  97.5 0.7 collective-permute-done.8
  98.3 0.8 broadcast_in_dim.184
  99.1 6.7 %all-to-all-start = ((bf16[16,48,256]{2,1,0:T(8,128)(2,1)}), bf16[16,48,256]{2,1,0:T(8,128)(2,1)S(1)}, u32[]{:S(2)}, u32[]{:S(2)}) async-start(bf16[16,48,256]{2,1,0:T(8,128)(2,1)} %bitcast.17), calls=%async_computation | async-start | bytes 786432 | tf_op jit(solution)/shard_map/all_to_all | solution.py:85
  105.8 9.5 %all-to-all-done = bf16[16,48,256]{2,1,0:T(8,128)(2,1)S(1)} async-done(((bf16[16,48,256]{2,1,0:T(8,128)(2,1)}), bf16[16,48,256]{2,1,0:T(8,128)(2,1)S(1)}, u32[]{:S(2)}, u32[]{:S(2)}) %all-to-all-start) | async-done | bytes 393248 | tf_op jit(solution)/shard_map/all_to_all | solution.py:85
  115.3 0.1 add_convert_fusion.6
  115.4 0.6 add_convert_fusion.2
  116.0 1.6 %fusion.10 = f32[256,512]{1,0:T(8,128)S(1)} fusion(bf16[512,256]{1,0:T(8,128)(2,1)S(1)} %bitcast.105, bf16[512,3072]{1,0:T(8,128)(2,1)} %all-gather.2.cloned.1.call-done), kind=kOutput, calls=%fused_computation.25 | convolution fusion | flops 134217728 | bytes 1310720 | tf_op jit(solution)/shard_map/dot_general | solution.py:96
  117.6 0.3 convolution_add_fusion.2
  118.0 0.3 convolution_add_fusion.1
  118.3 0.3 fusion
  118.6 0.8 add_convert_fusion.1
  (28 shorter events, 0.2 us)
Async XLA Ops:
  6.5 37.4 %copy-start = (bf16[1024,1024]{1,0:T(8,128)(2,1)S(1)}, bf16[1024,1024]{1,0:T(8,128)(2,1)}, u32[]{:S(2)}) copy-start(bf16[1024,1024]{1,0:T(8,128)(2,1)} %param.6) | copy-start | bytes 6291460
  6.5 76.0 %all-gather.2.cloned.1.call-start = ((), (), s32[]{:S(2)}) async-start(), calls=%async_computation.1 | async-start | bytes 3342336 | tf_op jit(solution)/shard_map/all_gather | solution.py:121
  8.4 0.7 copy-start.7
  9.9 34.0 %copy-start.2 = (bf16[256,1024]{1,0:T(8,128)(2,1)S(1)}, bf16[256,1024]{1,0:T(8,128)(2,1)}, u32[]{:S(2)}) copy-start(bf16[256,1024]{1,0:T(8,128)(2,1)} %param.5) | copy-start | bytes 1572868
  11.1 12.2 %collective-permute-start.2 = (bf16[272,1024]{1,0:T(8,128)(2,1)S(1)}, bf16[272,1024]{1,0:T(8,128)(2,1)}, u32[]{:S(2)}, u32[]{:S(2)}) collective-permute-start(bf16[272,1024]{1,0:T(8,128)(2,1)S(1)} %fusion.6), channel_id=1, source_target_pairs={{0,1},{1,2},{2,3},{3,0},{4,5},{5,6},{6,7},{7,4},{8,9},{9,10},{10,1... | collective-permute-start | bytes 1671176 | tf_op jit(solution)/shard_map/ppermute | solution.py:8
  15.0 26.5 %collective-permute-start.1 = (bf16[272,1024]{1,0:T(8,128)(2,1)S(1)}, bf16[272,1024]{1,0:T(8,128)(2,1)}, u32[]{:S(2)}, u32[]{:S(2)}) collective-permute-start(bf16[272,1024]{1,0:T(8,128)(2,1)S(1)} %fusion.6), channel_id=1, source_target_pairs={{0,2},{1,3},{2,0},{3,1},{4,6},{5,7},{6,4},{7,5},{8,10},{9,11},{10,... | collective-permute-start | bytes 1671176 | tf_op jit(solution)/shard_map/ppermute | solution.py:8
  19.4 23.2 %collective-permute-start = (bf16[272,1024]{1,0:T(8,128)(2,1)S(1)}, bf16[272,1024]{1,0:T(8,128)(2,1)}, u32[]{:S(2)}, u32[]{:S(2)}) collective-permute-start(bf16[272,1024]{1,0:T(8,128)(2,1)S(1)} %fusion.6), channel_id=1, source_target_pairs={{0,3},{1,0},{2,1},{3,2},{4,7},{5,4},{6,5},{7,6},{8,11},{9,8},{10,9... | collective-permute-start | bytes 1671176 | tf_op jit(solution)/shard_map/ppermute | solution.py:8
  24.4 21.8 %copy-start.4 = (bf16[256,1024]{1,0:T(8,128)(2,1)}, bf16[256,1024]{1,0:T(8,128)(2,1)S(1)}, u32[]{:S(2)}) copy-start(bf16[256,1024]{1,0:T(8,128)(2,1)S(1)} %slice.152) | copy-start | bytes 1572868
  42.6 3.6 %copy-start.5 = (bf16[256,1024]{1,0:T(8,128)(2,1)}, bf16[256,1024]{1,0:T(8,128)(2,1)S(1)}, u32[]{:S(2)}) copy-start(bf16[256,1024]{1,0:T(8,128)(2,1)S(1)} %slice.151) | copy-start | bytes 1572868
  43.9 2.3 %copy-start.6 = (bf16[256,1024]{1,0:T(8,128)(2,1)}, bf16[256,1024]{1,0:T(8,128)(2,1)S(1)}, u32[]{:S(2)}) copy-start(bf16[256,1024]{1,0:T(8,128)(2,1)S(1)} %slice.150) | copy-start | bytes 1572868
  43.9 8.3 %copy-start.8 = (s32[8,3]{0,1:T(4,128)S(1)}, s32[8,3]{0,1:T(4,128)}, u32[]{:S(2)}) copy-start(s32[8,3]{0,1:T(4,128)} %param.9) | copy-start | bytes 292
  46.2 9.0 %collective-permute-start.3 = (bf16[1024,512]{1,0:T(8,128)(2,1)}, bf16[1024,512]{1,0:T(8,128)(2,1)S(1)}, u32[]{:S(2)}, u32[]{:S(2)}) collective-permute-start(bf16[1024,512]{1,0:T(8,128)(2,1)} %convolution_convert_fusion), channel_id=1, source_target_pairs={{0,64},{64,0},{128,192},{192,128},{256,320},{320,256},{384,448},{4... | collective-permute-start | bytes 3145736 | tf_op jit(solution)/shard_map/ppermute | solution.py:12
  55.5 27.0 %copy-start.3 = (bf16[256,1024]{1,0:T(8,128)(2,1)S(1)}, bf16[256,1024]{1,0:T(8,128)(2,1)}, u32[]{:S(2)}) copy-start(bf16[256,1024]{1,0:T(8,128)(2,1)} %param.5) | copy-start | bytes 1572868
  55.6 15.9 %collective-permute-start.4 = (bf16[256,512]{1,0:T(8,128)(2,1)S(1)}, bf16[256,512]{1,0:T(8,128)(2,1)S(1)}, u32[]{:S(2)}, u32[]{:S(2)}) collective-permute-start(bf16[256,512]{1,0:T(8,128)(2,1)S(1)} %get-tuple-element.12), channel_id=1, source_target_pairs={{0,0},{64,64},{128,1},{192,65},{256,2},{320,66},{384,3},{448,67},{... | collective-permute-start | bytes 786440 | tf_op jit(solution)/shard_map/ppermute | solution.py:43
  56.4 19.1 %collective-permute-start.7 = (bf16[256,512]{1,0:T(8,128)(2,1)S(1)}, bf16[256,512]{1,0:T(8,128)(2,1)S(1)}, u32[]{:S(2)}, u32[]{:S(2)}) collective-permute-start(bf16[256,512]{1,0:T(8,128)(2,1)S(1)} %get-tuple-element.13), channel_id=1, source_target_pairs={{0,3},{64,67},{128,0},{192,64},{256,1},{320,65},{384,2},{448,66},{... | collective-permute-start | bytes 786440 | tf_op jit(solution)/shard_map/ppermute | solution.py:43
  64.9 10.8 %collective-permute-start.6 = (bf16[256,512]{1,0:T(8,128)(2,1)S(1)}, bf16[256,512]{1,0:T(8,128)(2,1)S(1)}, u32[]{:S(2)}, u32[]{:S(2)}) collective-permute-start(bf16[256,512]{1,0:T(8,128)(2,1)S(1)} %get-tuple-element.14), channel_id=1, source_target_pairs={{0,2},{64,66},{128,3},{192,67},{256,0},{320,64},{384,1},{448,65},{... | collective-permute-start | bytes 786440 | tf_op jit(solution)/shard_map/ppermute | solution.py:43
  69.3 13.1 %collective-permute-start.5 = (bf16[256,512]{1,0:T(8,128)(2,1)S(1)}, bf16[256,512]{1,0:T(8,128)(2,1)S(1)}, u32[]{:S(2)}, u32[]{:S(2)}) collective-permute-start(bf16[256,512]{1,0:T(8,128)(2,1)S(1)} %get-tuple-element.15), channel_id=1, source_target_pairs={{0,1},{64,65},{128,2},{192,66},{256,3},{320,67},{384,0},{448,64},{... | collective-permute-start | bytes 786440 | tf_op jit(solution)/shard_map/ppermute | solution.py:43
  86.4 11.8 %collective-permute-start.8 = (bf16[48,1024]{1,0:T(8,128)(2,1)S(1)}, bf16[48,1024]{1,0:T(8,128)(2,1)S(1)}, u32[]{:S(2)}, u32[]{:S(2)}) collective-permute-start(bf16[48,1024]{1,0:T(8,128)(2,1)S(1)} %pad_maximum_fusion.1), channel_id=1, source_target_pairs={{0,64},{64,0},{128,192},{192,128},{256,320},{320,256},{384,448},{4... | collective-permute-start | bytes 294920 | tf_op jit(solution)/shard_map/ppermute | solution.py:12
  99.1 16.3 %all-to-all-start = ((bf16[16,48,256]{2,1,0:T(8,128)(2,1)}), bf16[16,48,256]{2,1,0:T(8,128)(2,1)S(1)}, u32[]{:S(2)}, u32[]{:S(2)}) async-start(bf16[16,48,256]{2,1,0:T(8,128)(2,1)} %bitcast.17), calls=%async_computation | async-start | bytes 786432 | tf_op jit(solution)/shard_map/all_to_all | solution.py:85
  115.3 2.3 %copy-start.1 = (bf16[512,3072]{1,0:T(8,128)(2,1)S(1)}, bf16[512,3072]{1,0:T(8,128)(2,1)}, u32[]{:S(2)}) copy-start(bf16[512,3072]{1,0:T(8,128)(2,1)} %all-gather.2.cloned.1.call-done) | copy-start | bytes 9437188
Sparse Core Ops, SparseCore 0:
  9.4 73.0 all-gather.1
